TPU v7x, 32 devices: a whole 2x2x4 slice. The times are simulated.
32 devices in a mesh: wide: 8 (over y, x, core), narrow: 4 (over z).
Axes of the slice: x: 2, y: 2, z: 4, core: 2. Of those that a mesh axis runs over, the one named last changes fastest.
Arguments:
- tokens: bfloat16 [32, 1536, 768], P(('wide', 'narrow')), may hold values from -6 to 6
- lengths: int32 [8, 4], P('wide'), may hold values from 1 to 1536, 4608 in all within a row
- qkv_weight: bfloat16 [768, 3, 768], P(None, None, 'narrow'), may hold values from -0.3125 to 0.3125
- qkv_bias: bfloat16 [3, 768], P(None, 'narrow'), may hold values from -3 to 3
- out_weight: bfloat16 [768, 768], P('narrow'), may hold values from -2.5 to 2.5
- out_bias: bfloat16 [768], replicated, may hold values from -2 to 2
- norm1_gain: bfloat16 [768], replicated, may hold values from 0.099609375 to 1.8984375
- norm1_shift: bfloat16 [768], replicated, may hold values from -2 to 2
- up_weight: bfloat16 [768, 3072], P(None, 'narrow'), may hold values from -0.21875 to 0.21875
- up_bias: bfloat16 [3072], P('narrow'), may hold values from -2 to 2
- down_weight: bfloat16 [3072, 768], P('narrow'), may hold values from -0.109375 to 0.109375
- down_bias: bfloat16 [768], replicated, may hold values from -2 to 2
- norm2_gain: bfloat16 [768], replicated, may hold values from 0.099609375 to 1.8984375
- norm2_shift: bfloat16 [768], replicated, may hold values from -2 to 2
- cotangent: bfloat16 [32, 1536, 768], P(('wide', 'narrow')), may hold values from -6 to 6
Outputs:
- output: bfloat16 [32, 1536, 768], P(('wide', 'narrow'))
- input_grad: float32 [32, 1536, 768], P(('wide', 'narrow'))
- grad_qkv_weight: float32 [768, 3, 768], P(None, None, 'narrow')
- grad_qkv_bias: float32 [3, 768], P(None, 'narrow')
- grad_out_weight: float32 [768, 768], P('narrow')
- grad_out_bias: float32 [768], replicated
- grad_norm1_gain: float32 [768], replicated
- grad_norm1_shift: float32 [768], replicated
- grad_up_weight: float32 [768, 3072], P(None, 'narrow')
- grad_up_bias: float32 [3072], P('narrow')
- grad_down_weight: float32 [3072, 768], P('narrow')
- grad_down_bias: float32 [768], replicated
- grad_norm2_gain: float32 [768], replicated
- grad_norm2_shift: float32 [768], replicated
Inputs may be any that keep to these rules, and one draw needn't show every extreme that they name: The 4 lengths of each wide index sum to 4608; positions at or beyond a slot's length are keys that no query attends to.
All inputs are finite; a program needn't handle non-finite values.
Results may differ from a plain program's by a relative error of at most 0.018.
The roundings to bfloat16 on the way count: a program that leaves them out, or rounds other values in their place, can miss the bound.
Values may be sent and summed in bfloat16 or wider, within the bound.
No kernel may reach another device: no remote copies, remote signals or barrier semaphores. Data moves between devices by JAX's collectives and lax.ppermute only.
A program may use at most 256 MiB of HBM per device.

v0:
```python
import jax
import jax.numpy as jnp
from jax import lax
from jax.sharding import PartitionSpec as P

HEADS = 12
HD = 64


NORM_EPS = 1e-06
MASK_VALUE = -1000000000.0


def rotary_tables(capacity, head_dim):
    positions = jnp.arange(capacity).astype(jnp.float32)
    frequencies = 10000.0 ** (-2.0 * jnp.arange(head_dim // 2).astype(jnp.float32) / head_dim)
    angles = positions[:, None] * frequencies[None, :]
    return (jnp.cos(angles)[:, None, :], jnp.sin(angles)[:, None, :])


def rotate(values, cosine, sine):
    half_dim = values.shape[-1] // 2
    first_half = values[..., :half_dim]
    second_half = values[..., half_dim:]
    return jnp.concatenate(
        [first_half * cosine - second_half * sine, second_half * cosine + first_half * sine],
        axis=-1,
    )


def norm_forward(values, gain_vec, shift_vec):
    row_mean = jnp.mean(values, axis=-1, keepdims=True)
    centred = values - row_mean
    inv_std = lax.rsqrt(jnp.mean(centred * centred, axis=-1, keepdims=True) + NORM_EPS)
    normed = centred * inv_std
    return (normed * gain_vec + shift_vec, normed, inv_std)


def norm_backward(upstream, normed, inv_std, gain_vec):
    scaled = upstream * gain_vec
    inner = (
        scaled
        - jnp.mean(scaled, axis=-1, keepdims=True)
        - normed * jnp.mean(scaled * normed, axis=-1, keepdims=True)
    )
    gain_grad = jnp.sum(upstream * normed, axis=(0, 1))
    shift_grad = jnp.sum(upstream, axis=(0, 1))
    return (inv_std * inner, gain_grad, shift_grad)


def to_items(values, group_count):
    slot_count, capacity, head_count, head_dim = values.shape
    values = values.reshape(slot_count, capacity, group_count, head_count // group_count, head_dim)
    values = values.transpose(0, 2, 1, 3, 4)
    return values.reshape(slot_count * group_count, capacity, head_count // group_count, head_dim)


def from_items(values, group_count):
    item_count, capacity, group_heads, head_dim = values.shape
    values = values.reshape(item_count // group_count, group_count, capacity, group_heads, head_dim)
    values = values.transpose(0, 2, 1, 3, 4)
    return values.reshape(item_count // group_count, capacity, group_count * group_heads, head_dim)


def attend_forward(query_item, key_item, value_item, item_length, block_rows, score_scale):
    capacity = query_item.shape[0]
    live_keys = jnp.arange(capacity) < item_length

    def one_block(offset):
        query_block = lax.dynamic_slice_in_dim(query_item, offset, block_rows, 0)
        scores = (
            jnp.einsum("qhe,khe->hqk", query_block, key_item, preferred_element_type=jnp.float32)
            * score_scale
        )
        scores = jnp.where(live_keys[None, None, :], scores, MASK_VALUE)
        row_max = jnp.max(scores, axis=-1, keepdims=True)
        exponentials = jnp.exp(scores - row_max)
        denominator = jnp.sum(exponentials, axis=-1, keepdims=True)
        weights = (exponentials / denominator).astype(jnp.bfloat16)
        context = jnp.einsum(
            "hqk,khe->qhe", weights, value_item, preferred_element_type=jnp.float32
        )
        return (context, (row_max + jnp.log(denominator))[..., 0])

    offsets = jnp.arange(capacity // block_rows) * block_rows
    context, log_sums = lax.map(one_block, offsets)
    return (context.reshape(query_item.shape), log_sums)


def attend_backward(
    query_item, key_item, value_item, grad_item, log_sums, item_length, block_rows, score_scale
):
    capacity = query_item.shape[0]
    live_keys = jnp.arange(capacity) < item_length

    def one_block(carry, inputs):
        key_grad, value_grad = carry
        offset, block_sums = inputs
        query_block = lax.dynamic_slice_in_dim(query_item, offset, block_rows, 0)
        grad_block = lax.dynamic_slice_in_dim(grad_item, offset, block_rows, 0)
        scores = (
            jnp.einsum("qhe,khe->hqk", query_block, key_item, preferred_element_type=jnp.float32)
            * score_scale
        )
        scores = jnp.where(live_keys[None, None, :], scores, MASK_VALUE)
        weights = jnp.exp(scores - block_sums[..., None])
        weight_grad = jnp.einsum(
            "qhe,khe->hqk", grad_block, value_item, preferred_element_type=jnp.float32
        )
        row_dot = jnp.sum(weight_grad * weights, axis=-1, keepdims=True)
        score_grad = (weights * (weight_grad - row_dot)).astype(jnp.bfloat16)
        query_grad = (
            jnp.einsum("hqk,khe->qhe", score_grad, key_item, preferred_element_type=jnp.float32)
            * score_scale
        )
        key_grad = (
            key_grad
            + jnp.einsum(
                "hqk,qhe->khe", score_grad, query_block, preferred_element_type=jnp.float32
            )
            * score_scale
        )
        value_grad = value_grad + jnp.einsum(
            "hqk,qhe->khe",
            weights.astype(jnp.bfloat16),
            grad_block,
            preferred_element_type=jnp.float32,
        )
        return ((key_grad, value_grad), query_grad)

    offsets = jnp.arange(capacity // block_rows) * block_rows
    zero_rows = jnp.zeros(key_item.shape, jnp.float32)
    (key_grad, value_grad), query_grad = lax.scan(
        one_block, (zero_rows, zero_rows), (offsets, log_sums)
    )
    return (query_grad.reshape(key_item.shape), key_grad, value_grad)


def shards(
    tokens,
    lengths,
    qkv_weight,
    qkv_bias,
    out_weight,
    out_bias,
    norm1_gain,
    norm1_shift,
    up_weight,
    up_bias,
    down_weight,
    down_bias,
    norm2_gain,
    norm2_shift,
    cotangent,
):
    narrow_size = lax.axis_size("narrow")
    slot_dev, capacity, features = tokens.shape
    group_heads = HEADS // narrow_size
    score_scale = HD ** (-0.5)
    block_rows = min(capacity, 512)
    cosine, sine = rotary_tables(capacity, HD)
    all_lengths = lengths.reshape(-1)
    gain_one = norm1_gain.astype(jnp.float32)
    shift_one = norm1_shift.astype(jnp.float32)
    gain_two = norm2_gain.astype(jnp.float32)
    shift_two = norm2_shift.astype(jnp.float32)
    qkv_local, qkv_bias_local, out_local = (qkv_weight, qkv_bias, out_weight)
    up_local, up_bias_local, down_local = (up_weight, up_bias, down_weight)
    row_tokens = lax.all_gather(tokens, "narrow", axis=0, tiled=True)
    slot_count = row_tokens.shape[0]
    projected = jnp.einsum(
        "scd,dje->scje", row_tokens, qkv_local, preferred_element_type=jnp.float32
    ) + qkv_bias_local.astype(jnp.float32)
    head_count = projected.shape[3] // HD
    group_count = head_count // group_heads
    head_shape = (slot_count, capacity, head_count, HD)
    queries = rotate(projected[:, :, 0].reshape(head_shape), cosine, sine).astype(jnp.bfloat16)
    key_rows = rotate(projected[:, :, 1].reshape(head_shape), cosine, sine).astype(jnp.bfloat16)
    value_rows = projected[:, :, 2].reshape(head_shape).astype(jnp.bfloat16)
    item_lengths = jnp.repeat(all_lengths, group_count)
    query_items = to_items(queries, group_count)
    key_items = to_items(key_rows, group_count)
    value_items = to_items(value_rows, group_count)

    def forward_item(item):
        return attend_forward(item[0], item[1], item[2], item[3], block_rows, score_scale)

    context_items, log_sums = lax.map(
        forward_item, (query_items, key_items, value_items, item_lengths)
    )
    context = (
        from_items(context_items, group_count)
        .reshape(slot_count, capacity, head_count * HD)
        .astype(jnp.bfloat16)
    )
    attn_terms = jnp.einsum("scd,de->sce", context, out_local, preferred_element_type=jnp.float32)
    attended = lax.psum_scatter(attn_terms, "narrow", scatter_dimension=0, tiled=True)
    own_tokens = tokens.astype(jnp.float32)
    hidden, normed_one, inv_one = norm_forward(
        own_tokens + attended + out_bias.astype(jnp.float32), gain_one, shift_one
    )
    hidden_low = hidden.astype(jnp.bfloat16)
    hidden_rows = lax.all_gather(hidden_low, "narrow", axis=0, tiled=True)
    upward = jnp.einsum(
        "scd,df->scf", hidden_rows, up_local, preferred_element_type=jnp.float32
    ) + up_bias_local.astype(jnp.float32)
    active = jax.nn.gelu(upward, approximate=False).astype(jnp.bfloat16)
    down_terms = jnp.einsum("scf,fd->scd", active, down_local, preferred_element_type=jnp.float32)
    downward = lax.psum_scatter(down_terms, "narrow", scatter_dimension=0, tiled=True)
    output_value, normed_two, inv_two = norm_forward(
        hidden + downward + down_bias.astype(jnp.float32), gain_two, shift_two
    )
    output = output_value.astype(jnp.bfloat16)
    pre_two_grad, gain_two_grad, shift_two_grad = norm_backward(
        cotangent.astype(jnp.float32), normed_two, inv_two, gain_two
    )
    down_bias_grad = jnp.sum(pre_two_grad, axis=(0, 1))
    pre_two_low = pre_two_grad.astype(jnp.bfloat16)
    down_grad_rows = lax.all_gather(pre_two_low, "narrow", axis=0, tiled=True)
    down_grad = jnp.einsum(
        "scf,scd->fd", active, down_grad_rows, preferred_element_type=jnp.float32
    )
    active_grad = jnp.einsum(
        "scd,fd->scf", down_grad_rows, down_local, preferred_element_type=jnp.float32
    )
    ignored_value, gelu_pull = jax.vjp(lambda inner: jax.nn.gelu(inner, approximate=False), upward)
    upward_grad = gelu_pull(active_grad)[0]
    up_bias_grad = jnp.sum(upward_grad, axis=(0, 1))
    upward_low = upward_grad.astype(jnp.bfloat16)
    up_grad = jnp.einsum("scd,scf->df", hidden_rows, upward_low, preferred_element_type=jnp.float32)
    hidden_terms = jnp.einsum(
        "scf,df->scd", upward_low, up_local, preferred_element_type=jnp.float32
    )
    hidden_grad = lax.psum_scatter(hidden_terms, "narrow", scatter_dimension=0, tiled=True)
    pre_one_grad, gain_one_grad, shift_one_grad = norm_backward(
        hidden_grad + pre_two_grad, normed_one, inv_one, gain_one
    )
    out_bias_grad = jnp.sum(pre_one_grad, axis=(0, 1))
    pre_one_low = pre_one_grad.astype(jnp.bfloat16)
    out_grad_rows = lax.all_gather(pre_one_low, "narrow", axis=0, tiled=True)
    out_grad = jnp.einsum("scd,sce->de", context, out_grad_rows, preferred_element_type=jnp.float32)
    context_grad = jnp.einsum(
        "sce,de->scd", out_grad_rows, out_local, preferred_element_type=jnp.float32
    ).astype(jnp.bfloat16)
    grad_items = to_items(context_grad.reshape(head_shape), group_count)

    def backward_item(item):
        return attend_backward(
            item[0], item[1], item[2], item[3], item[4], item[5], block_rows, score_scale
        )

    query_grad, key_grad, value_grad = lax.map(
        backward_item, (query_items, key_items, value_items, grad_items, log_sums, item_lengths)
    )
    flat_shape = (slot_count, capacity, head_count * HD)
    query_grad = rotate(from_items(query_grad, group_count), cosine, -sine).reshape(flat_shape)
    key_grad = rotate(from_items(key_grad, group_count), cosine, -sine).reshape(flat_shape)
    value_grad = from_items(value_grad, group_count).reshape(flat_shape)
    projected_grad = jnp.stack([query_grad, key_grad, value_grad], axis=2)
    qkv_bias_grad = jnp.sum(projected_grad, axis=(0, 1))
    projected_low = projected_grad.astype(jnp.bfloat16)
    qkv_grad = jnp.einsum(
        "scd,scje->dje", row_tokens, projected_low, preferred_element_type=jnp.float32
    )
    input_terms = jnp.einsum(
        "scje,dje->scd", projected_low, qkv_local, preferred_element_type=jnp.float32
    )
    input_part = lax.psum_scatter(
        input_terms.astype(jnp.bfloat16), "narrow", scatter_dimension=0, tiled=True
    ).astype(jnp.float32)
    input_grad = input_part + pre_one_grad
    small_grads = lax.psum(
        (
            gain_one_grad,
            shift_one_grad,
            gain_two_grad,
            shift_two_grad,
            out_bias_grad,
            down_bias_grad,
        ),
        "narrow",
    )
    summed = lax.psum(
        (
            qkv_grad,
            qkv_bias_grad,
            out_grad,
            small_grads[4],
            small_grads[0],
            small_grads[1],
            up_grad,
            up_bias_grad,
            down_grad,
            small_grads[5],
            small_grads[2],
            small_grads[3],
        ),
        "wide",
    )
    return (
        output,
        input_grad,
        summed[0],
        summed[1],
        summed[2],
        summed[3],
        summed[4],
        summed[5],
        summed[6],
        summed[7],
        summed[8],
        summed[9],
        summed[10],
        summed[11],
    )


def solution(mesh):
    placed = (
        P(("wide", "narrow"), None, None),
        P("wide", None),
        P(None, None, "narrow"),
        P(None, "narrow"),
        P("narrow", None),
        P(),
        P(),
        P(),
        P(None, "narrow"),
        P("narrow"),
        P("narrow", None),
        P(),
        P(),
        P(),
        P(("wide", "narrow"), None, None),
    )
    return jax.shard_map(
        shards,
        mesh=mesh,
        in_specs=placed,
        out_specs=(
            P(("wide", "narrow"), None, None),
            P(("wide", "narrow"), None, None),
            P(None, None, "narrow"),
            P(None, "narrow"),
            P("narrow", None),
            P(),
            P(),
            P(),
            P(None, "narrow"),
            P("narrow"),
            P("narrow", None),
            P(),
            P(),
            P(),
        ),
        check_vma=False,
    )
```

profile of v0, /device:TPU:0, one launch (start us, length us, event | category | flops | bytes accessed | tf_op | source)
XLA Modules:
  0.0 2779.0 jit_solution(16459754968414012674)
XLA Ops:
  11.8 167.4 %all-gather.5.cloned.1.call-done = bf16[4,1536,768]{2,1,0:T(8,128)(2,1)} async-done(((bf16[1,1536,768]{2,1,0:T(8,128)(2,1)}), bf16[4,1536,768]{2,1,0:T(8,128)(2,1)}) %all-gather.5.cloned.1.call-update) | async-done | bytes 9437200 | tf_op jit(solution)/shard_map/all_gather | solution.py:169
  179.1 12.5 fusion.47
  204.4 152.3 %while.61 = (s32[]{:T(128)}, bf16[4,1536,3,64]{1,3,2,0:T(8,128)(2,1)}, f32[4,3,3,512]{3,2,1,0:T(4,128)}, bf16[4,1536,3,64]{1,3,2,0:T(8,128)(2,1)}, bf16[4,1536,3...) while((s32[]{:T(128)}, ...), condition=%wide.region_5.6_spmd.clone, body=%wide.region_0.5_spmd.sunk.clone | while | flops 632291328 | bytes 37272460 | solution.py:188
  207.4 30.9 %while.60 = (s32[]{:T(128)}, bf16[3,512,3,64]{1,3,2,0:T(8,128)(2,1)S(1)}, f32[3,3,512]{2,1,0:T(4,128)}, s32[3]{0:T(128)S(1)}, bf16[1536,3,64]{0,2,1:T(8,128)(2,1...) while((s32[]{:T(128)}, ...), condition=%wide.region_4.4_spmd.clone, body=%wide.region_1.3_spmd.clone.sunk | while | flops 632291328 | bytes 30144168 | solution.py:86
  245.5 30.9 %while.60 = (s32[]{:T(128)}, bf16[3,512,3,64]{1,3,2,0:T(8,128)(2,1)S(1)}, f32[3,3,512]{2,1,0:T(4,128)}, s32[3]{0:T(128)S(1)}, bf16[1536,3,64]{0,2,1:T(8,128)(2,1...) while((s32[]{:T(128)}, ...), condition=%wide.region_4.4_spmd.clone, body=%wide.region_1.3_spmd.clone.sunk | while | flops 632291328 | bytes 30144168 | solution.py:86
  283.5 30.9 %while.60 = (s32[]{:T(128)}, bf16[3,512,3,64]{1,3,2,0:T(8,128)(2,1)S(1)}, f32[3,3,512]{2,1,0:T(4,128)}, s32[3]{0:T(128)S(1)}, bf16[1536,3,64]{0,2,1:T(8,128)(2,1...) while((s32[]{:T(128)}, ...), condition=%wide.region_4.4_spmd.clone, body=%wide.region_1.3_spmd.clone.sunk | while | flops 632291328 | bytes 30144168 | solution.py:86
  321.6 30.9 %while.60 = (s32[]{:T(128)}, bf16[3,512,3,64]{1,3,2,0:T(8,128)(2,1)S(1)}, f32[3,3,512]{2,1,0:T(4,128)}, s32[3]{0:T(128)S(1)}, bf16[1536,3,64]{0,2,1:T(8,128)(2,1...) while((s32[]{:T(128)}, ...), condition=%wide.region_4.4_spmd.clone, body=%wide.region_1.3_spmd.clone.sunk | while | flops 632291328 | bytes 30144168 | solution.py:86
  356.7 10.8 fusion.79
  368.2 311.4 %reduce-scatter.5.cloned.1.call-done = f32[1,1536,768]{2,1,0:T(8,128)} async-done(((f32[4,1536,768]{2,1,0:T(8,128)}), f32[1,1536,768]{2,1,0:T(8,128)}) %reduce-scatter.5.cloned.1.call-update) | async-done | bytes 4718608 | tf_op jit(solution)/shard_map/reduce_scatter | solution.py:197
  687.0 167.9 %all-gather.7.cloned.1.call-done = bf16[4,1536,768]{2,1,0:T(8,128)(2,1)} async-done(((bf16[1,1536,768]{2,1,0:T(8,128)(2,1)}), bf16[4,1536,768]{2,1,0:T(8,128)(2,1)}) %all-gather.7.cloned.1.call-update) | async-done | bytes 9437200 | tf_op jit(solution)/shard_map/all_gather | solution.py:203
  855.0 19.3 fusion.62
  874.3 46.0 %multiply_convert_fusion.1 = (bf16[4,1536,768]{2,1,0:T(8,128)(2,1)S(1)}, f32[4,1536,768]{2,1,0:T(8,128)}) fusion(f32[4,1536,768]{2,1,0:T(8,128)} %get-tuple-element.438, f32[768]{0:T(1024)S(1)} %convert_element_type.166, u8[1536,768]{1,0:T(8,128)(4,1)S(1)} %get-tuple-element.302, u8[1536,768]{1,0:T(8,128)(4,1)S(1)} %get-tuple-element.301), kind=kLoop, calls=%fused_computation.65 | loop fusion | flops 335020032 | bytes 49548288 | tf_op jit(solution)/shard_map/convert_element_type | solution.py:207
  923.9 10.5 fusion.71
  934.5 11.2 all-gather.9.cloned.1.call-start
  945.7 300.9 %reduce-scatter.7.cloned.1.call-done = f32[1,1536,768]{2,1,0:T(8,128)} async-done(((f32[4,1536,768]{2,1,0:T(8,128)}), f32[1,1536,768]{2,1,0:T(8,128)}) %reduce-scatter.7.cloned.1.call-update) | async-done | bytes 4718608 | tf_op jit(solution)/shard_map/reduce_scatter | solution.py:209
  1263.6 168.0 %all-gather.9.cloned.1.call-done = bf16[4,1536,768]{2,1,0:T(8,128)(2,1)} async-done(((bf16[1,1536,768]{2,1,0:T(8,128)(2,1)}), bf16[4,1536,768]{2,1,0:T(8,128)(2,1)}) %all-gather.9.cloned.1.call-update) | async-done | bytes 9437200 | tf_op jit(solution)/shard_map/all_gather | solution.py:219
  1431.6 25.3 fusion.91
  1456.8 14.4 fusion.59
  1471.3 312.1 %reduce-scatter.9.cloned.1.call-done = f32[1,1536,768]{2,1,0:T(8,128)} async-done(((f32[4,1536,768]{2,1,0:T(8,128)}), f32[1,1536,768]{2,1,0:T(8,128)}) %reduce-scatter.9.cloned.1.call-update) | async-done | bytes 4718608 | tf_op jit(solution)/shard_map/reduce_scatter | solution.py:234
  1783.4 7.0 multiply_reduce_fusion.1
  1798.7 168.0 %all-gather.11.cloned.1.call-done = bf16[4,1536,768]{2,1,0:T(8,128)(2,1)} async-done(((bf16[1,1536,768]{2,1,0:T(8,128)(2,1)}), bf16[4,1536,768]{2,1,0:T(8,128)(2,1)}) %all-gather.11.cloned.1.call-update) | async-done | bytes 9437200 | tf_op jit(solution)/shard_map/all_gather | solution.py:240
  1966.7 6.9 convolution_convert_fusion
  1979.2 481.6 %while.63 = (s32[]{:T(128)}, f32[4,1536,3,64]{1,3,2,0:T(8,128)}, f32[4,1536,3,64]{1,3,2,0:T(8,128)}, f32[4,1536,3,64]{1,3,2,0:T(8,128)}, f32[4,3,3,512]{3,2,1,0:...) while((s32[]{:T(128)}, f32[4,1536,3,64]{1,3,2,0:T(8,128)}, ...), condition=%wide.region_21.22_spmd.clone, body=%wide.region_17.21_spmd.sunk.clone | while | flops 1532755968 | bytes 175250576 | solution.py:252
  1987.0 104.4 %while.62 = (s32[]{:T(128)}, f32[1536,3,64]{0,2,1:T(8,128)S(1)}, f32[1536,3,64]{0,2,1:T(8,128)S(1)}, f32[3,512,3,64]{1,3,2,0:T(8,128)}, s32[3]{0:T(128)S(1)}, /*...) while((s32[]{:T(128)}, f32[1536,3,64]{0,2,1:T(8,128)S(1)}, ...), condition=%wide.region_20.20_spmd.clone, body=%wide.region_18.19_spmd.clone.sunk | while | flops 1532755968 | bytes 135104288 | solution.py:133
  1994.7 6.6 multiply_reduce_fusion.7
  2001.2 9.4 multiply_convert_fusion.3
  2016.8 5.0 fusion.138
  2029.5 6.6 multiply_reduce_fusion.7
  2036.1 9.4 multiply_convert_fusion.3
  2064.3 6.5 multiply_reduce_fusion.7
  2070.8 9.4 multiply_convert_fusion.3
  2107.3 104.4 %while.62 = (s32[]{:T(128)}, f32[1536,3,64]{0,2,1:T(8,128)S(1)}, f32[1536,3,64]{0,2,1:T(8,128)S(1)}, f32[3,512,3,64]{1,3,2,0:T(8,128)}, s32[3]{0:T(128)S(1)}, /*...) while((s32[]{:T(128)}, f32[1536,3,64]{0,2,1:T(8,128)S(1)}, ...), condition=%wide.region_20.20_spmd.clone, body=%wide.region_18.19_spmd.clone.sunk | while | flops 1532755968 | bytes 135104288 | solution.py:133
  2115.0 6.6 multiply_reduce_fusion.7
  2121.6 9.4 multiply_convert_fusion.3
  2149.8 6.6 multiply_reduce_fusion.7
  2156.4 9.4 multiply_convert_fusion.3
  2184.7 6.5 multiply_reduce_fusion.7
  2191.2 9.4 multiply_convert_fusion.3
  2227.6 104.4 %while.62 = (s32[]{:T(128)}, f32[1536,3,64]{0,2,1:T(8,128)S(1)}, f32[1536,3,64]{0,2,1:T(8,128)S(1)}, f32[3,512,3,64]{1,3,2,0:T(8,128)}, s32[3]{0:T(128)S(1)}, /*...) while((s32[]{:T(128)}, f32[1536,3,64]{0,2,1:T(8,128)S(1)}, ...), condition=%wide.region_20.20_spmd.clone, body=%wide.region_18.19_spmd.clone.sunk | while | flops 1532755968 | bytes 135104288 | solution.py:133
  2235.3 6.6 multiply_reduce_fusion.7
  2241.8 9.4 multiply_convert_fusion.3
  2270.1 6.6 multiply_reduce_fusion.7
  2276.7 9.4 multiply_convert_fusion.3
  2304.9 6.5 multiply_reduce_fusion.7
  2311.4 9.4 multiply_convert_fusion.3
  2347.8 104.4 %while.62 = (s32[]{:T(128)}, f32[1536,3,64]{0,2,1:T(8,128)S(1)}, f32[1536,3,64]{0,2,1:T(8,128)S(1)}, f32[3,512,3,64]{1,3,2,0:T(8,128)}, s32[3]{0:T(128)S(1)}, /*...) while((s32[]{:T(128)}, f32[1536,3,64]{0,2,1:T(8,128)S(1)}, ...), condition=%wide.region_20.20_spmd.clone, body=%wide.region_18.19_spmd.clone.sunk | while | flops 1532755968 | bytes 135104288 | solution.py:133
  2355.5 6.6 multiply_reduce_fusion.7
  2362.1 9.4 multiply_convert_fusion.3
  2390.4 6.6 multiply_reduce_fusion.7
  2396.9 9.4 multiply_convert_fusion.3
  2425.2 6.5 multiply_reduce_fusion.7
  2431.7 9.4 multiply_convert_fusion.3
  2460.8 6.5 multiply_subtract_fusion.1
  2473.9 10.2 bitcast_convert_fusion
  2484.2 15.1 convolution_bitcast_fusion
  2499.4 14.0 fusion.64
  2513.4 6.5 convolution_bitcast_fusion.1
  2520.0 6.8 fusion.67
  2527.6 19.1 all-reduce.2
  2546.7 5.9 fusion.41
  2552.6 23.8 all-reduce
  2576.5 68.3 %reduce-scatter.11.cloned.1.call-done = bf16[1,1536,768]{2,1,0:T(8,128)(2,1)} async-done(((bf16[4,1536,768]{2,1,0:T(8,128)(2,1)}), bf16[1,1536,768]{2,1,0:T(8,128)(2,1)}) %reduce-scatter.11.cloned.1.call-update) | async-done | bytes 2359312 | tf_op jit(solution)/shard_map/reduce_scatter | solution.py:268
  2644.8 5.7 convert_add_fusion
  2650.5 113.9 %all-reduce.5.cloned.1.call-done = (f32[768,3,192]{0,2,1:T(8,128)}, f32[192,768]{1,0:T(8,128)}, f32[768,768]{1,0:T(8,128)}, f32[768,768]{1,0:T(8,128)}) async-done(((f32[768,3,192]{0,2,1:T(8,128)}, f32[192,768]{1,0:T(8,128)}, f32[768,768]{1,0:T(8,128)}, f32[768,768]{1,0:T(8,128)}), (f32[768,3,192]{0,2,1:T(8,128)}, f32[192,768]{1,0:T(8,128)}, f32[768,768]{1,0:T(8,128)}, ...) | async-done | bytes 7077904 | tf_op jit(solution)/shard_map/psum | solution.py:283
  (481 shorter events, 463.5 us)
Async XLA Ops:
  7.2 847.8 %copy-start = (bf16[768,768]{1,0:T(8,128)(2,1)S(1)}, bf16[768,768]{1,0:T(8,128)(2,1)}, u32[]{:S(2)}) copy-start(bf16[768,768]{1,0:T(8,128)(2,1)} %param.31) | copy-start | bytes 3538948
  7.2 171.9 %copy-start.36 = (bf16[768,3,192]{0,2,1:T(8,128)(2,1)S(1)}, bf16[768,3,192]{0,2,1:T(8,128)(2,1)}, u32[]{:S(2)}) copy-start(bf16[768,3,192]{0,2,1:T(8,128)(2,1)} %param.25) | copy-start | bytes 2654212
  7.2 171.9 %all-gather.5.cloned.1.call-start = ((), (), s32[]{:S(2)}) async-start(), calls=%async_computation.4 | async-start | bytes 11796480 | tf_op jit(solution)/shard_map/all_gather | solution.py:169
  7.9 671.7 %reduce-scatter.5.cloned.1.call-start = ((), (), s32[]{:S(2)}) async-start(), calls=%async_computation.5 | async-start | bytes 23592960 | tf_op jit(solution)/shard_map/reduce_scatter | solution.py:197
  11.8 188.6 %copy-start.19 = (f32[1536,32]{0,1:T(8,128)}, f32[1536,32]{0,1:T(8,128)S(1)}, u32[]{:S(2)}) copy-start(f32[1536,32]{0,1:T(8,128)S(1)} %get-tuple-element.437) | copy-start | bytes 589828
  367.5 312.2 %copy-start.13 = (bf16[1,1536,768]{2,1,0:T(8,128)(2,1)S(1)}, bf16[1,1536,768]{2,1,0:T(8,128)(2,1)}, u32[]{:S(2)}) copy-start(bf16[1,1536,768]{2,1,0:T(8,128)(2,1)} %param.23) | copy-start | bytes 7077892
  367.5 487.4 %all-gather.7.cloned.1.call-start = ((), (), s32[]{:S(2)}) async-start(), calls=%async_computation.6 | async-start | bytes 11796480 | tf_op jit(solution)/shard_map/all_gather | solution.py:203
  687.0 559.7 %reduce-scatter.7.cloned.1.call-start = ((), (), s32[]{:S(2)}) async-start(), calls=%async_computation.7 | async-start | bytes 23592960 | tf_op jit(solution)/shard_map/reduce_scatter | solution.py:209
  874.3 49.7 %copy-start.35 = (bf16[768,768]{1,0:T(8,128)(2,1)S(1)}, bf16[768,768]{1,0:T(8,128)(2,1)}, u32[]{:S(2)}) copy-start(bf16[768,768]{1,0:T(8,128)(2,1)} %param.33) | copy-start | bytes 3538948
  934.5 11.2 copy-start.32
  934.5 11.2 copy-start.33
  934.5 11.2 copy-start.34
  934.5 497.1 %all-gather.9.cloned.1.call-start = ((), (), s32[]{:S(2)}) async-start(), calls=%async_computation.8 | async-start | bytes 11796480 | tf_op jit(solution)/shard_map/all_gather | solution.py:219
  1263.6 519.8 %reduce-scatter.9.cloned.1.call-start = ((), (), s32[]{:S(2)}) async-start(), calls=%async_computation.9 | async-start | bytes 23592960 | tf_op jit(solution)/shard_map/reduce_scatter | solution.py:234
  1471.3 495.4 %all-gather.11.cloned.1.call-start = ((), (), s32[]{:S(2)}) async-start(), calls=%async_computation.10 | async-start | bytes 11796480 | tf_op jit(solution)/shard_map/all_gather | solution.py:240
  1797.0 169.7 %copy-start.20 = (bf16[192,768]{1,0:T(8,128)(2,1)S(1)}, bf16[192,768]{1,0:T(8,128)(2,1)}, u32[]{:S(2)}) copy-start(bf16[192,768]{1,0:T(8,128)(2,1)} %param.27) | copy-start | bytes 884740
  1798.7 846.1 %reduce-scatter.11.cloned.1.call-start = ((), (), s32[]{:S(2)}) async-start(), calls=%async_computation.11 | async-start | bytes 11796480 | tf_op jit(solution)/shard_map/reduce_scatter | solution.py:268
  1973.5 5.6 copy-start.39
  1979.6 7.4 copy-start.15
  1994.7 6.6 copy-start.2
  2010.6 3.9 copy-start.3
  2029.5 6.6 copy-start.2
  2045.5 3.9 copy-start.3
  2064.3 6.5 copy-start.2
  2080.2 3.8 copy-start.3
  2093.1 6.9 copy-start.16
  2099.9 7.3 copy-start.15
  2115.0 6.6 copy-start.2
  2131.0 3.9 copy-start.3
  2149.8 6.6 copy-start.2
  2165.8 3.9 copy-start.3
  2184.6 6.5 copy-start.2
  2213.4 6.8 copy-start.16
  2220.2 7.3 copy-start.15
  2235.3 6.6 copy-start.2
  2251.2 3.9 copy-start.3
  2270.1 6.6 copy-start.2
  2286.1 3.9 copy-start.3
  2304.9 6.5 copy-start.2
  2333.6 6.8 copy-start.16
  2340.5 7.3 copy-start.15
  2355.5 6.6 copy-start.2
  2371.5 3.9 copy-start.3
  2390.4 6.6 copy-start.2
  2406.3 3.9 copy-start.3
  2425.2 6.5 copy-start.2
  2453.9 6.9 copy-start.16
  2467.3 6.3 slice-start.4
  2469.9 4.1 copy-start.37
  2484.1 280.3 %all-reduce.5.cloned.1.call-start = ((), (), s32[]{:S(2)}) async-start(), calls=%async_computation.12 | async-start | bytes 14155776 | tf_op jit(solution)/shard_map/psum | solution.py:283
  2484.2 35.7 %slice-start = ((s8[4718592]{0:T(1024)(128)(4,1)}), s8[4194304]{0:T(1024)(128)(4,1)S(1)}, s32[]{:S(2)}) async-start(s8[4718592]{0:T(1024)(128)(4,1)} %bitcast.204), calls=%async_computation.13 | async-start | bytes 8388608
  2484.2 35.7 %slice-start.2 = ((s8[4718592]{0:T(1024)(128)(4,1)}), s8[4194304]{0:T(1024)(128)(4,1)S(1)}, s32[]{:S(2)}) async-start(s8[4718592]{0:T(1024)(128)(4,1)} %bitcast.209), calls=%async_computation.15 | async-start | bytes 8388608
  2484.2 35.7 %slice-start.6 = ((s8[4718592]{0:T(1024)(128)(4,1)}), s8[4194304]{0:T(1024)(128)(4,1)S(1)}, s32[]{:S(2)}) async-start(s8[4718592]{0:T(1024)(128)(4,1)} %bitcast.216), calls=%async_computation.19 | async-start | bytes 8388608
  2484.2 35.7 %slice-start.8 = ((s8[9437184]{0:T(1024)(128)(4,1)}), s8[4194304]{0:T(1024)(128)(4,1)S(1)}, s32[]{:S(2)}) async-start(s8[9437184]{0:T(1024)(128)(4,1)} %bitcast.222), calls=%async_computation.21 | async-start | bytes 8388608
  2484.2 35.7 %slice-start.9 = ((s8[9437184]{0:T(1024)(128)(4,1)}), s8[4194304]{0:T(1024)(128)(4,1)S(1)}, s32[]{:S(2)}) async-start(s8[9437184]{0:T(1024)(128)(4,1)} %bitcast.222), calls=%async_computation.22 | async-start | bytes 8388608
  2499.3 14.1 copy-start.14
  2499.3 20.6 slice-start.1
  2499.3 20.6 slice-start.3
  2499.3 20.6 slice-start.7
  2499.3 20.6 slice-start.10
  2546.7 5.9 copy-start.27
  2764.5 5.0 copy-start.18
  2764.5 6.4 copy-start.17
  2767.4 4.8 copy-start.1
  (27 other events, 52.7 us)
Sparse Core Ops, SparseCore 0:
  9.6 169.4 all-gather.4
  367.6 311.9 reduce-scatter.4
  687.1 167.8 all-gather.6
  934.6 311.9 reduce-scatter.6
  1263.7 167.8 all-gather.8
  1471.4 311.9 reduce-scatter.8
  1798.8 167.8 all-gather.10
  2484.2 160.5 reduce-scatter.10
  2650.1 114.3 all-reduce.4
where the time goes:
time: 2790 us; the launch traced here: 2780 us
  waiting for transfers between devices  1780 us (64%)
  matrix products  459 us (16%)
  other arithmetic  266 us (10%)
  local copies, waits for them, and re-layouts  157 us (6%)
  loops' own time  49.4 us (2%)
  blocking collectives  42.9 us (2%)
    reduce_scatter x1, waiting for transfers between devices, shards(): lax.psum_scatter(hidden_terms, 'narrow', scatter_dimension=0, tiled=True)  312 us
    reduce_scatter x1, waiting for transfers between devices, shards(): lax.psum_scatter(attn_terms, 'narrow', scatter_dimension=0, tiled=True)  311 us
    reduce_scatter x1, waiting for transfers between devices, shards(): lax.psum_scatter(down_terms, 'narrow', scatter_dimension=0, tiled=True)  301 us
    all_gather x1, waiting for transfers between devices, shards(): down_grad_rows = lax.all_gather(pre_two_low, 'narrow', axis=0, tiled=True)  168 us
    all_gather x1, waiting for transfers between devices, shards(): out_grad_rows = lax.all_gather(pre_one_low, 'narrow', axis=0, tiled=True)  168 us
    all_gather x1, waiting for transfers between devices, shards(): hidden_rows = lax.all_gather(hidden_low, 'narrow', axis=0, tiled=True)  168 us
    all_gather x1, waiting for transfers between devices, shards(): row_tokens = lax.all_gather(tokens, 'narrow', axis=0, tiled=True)  167 us
    psum x1, waiting for transfers between devices, shards(): lax.psum((qkv_grad, qkv_bias_grad, out_grad, small_grads[4], small_grads[...  114 us
  transfers between devices with their start and end apart: 9, of which 9 were waited for; matrix products, arithmetic and copies ran while one was open for 2% of the time, Pallas kernels for 0%

commit v1 on v0

v1 whole, which is shorter than its diff:
```python
import functools
import jax
import jax.numpy as jnp
from jax import lax
from jax.experimental import pallas as pl
from jax.experimental.pallas import tpu as pltpu
from jax.sharding import PartitionSpec as P

bf = jnp.bfloat16
f32 = jnp.float32
LOG2E = 1.4426950408889634
HEADS = 12
HD = 64


def dg(a, b, ca, cb):
    return lax.dot_general(a, b, (((ca,), (cb,)), ((), ())), preferred_element_type=f32)


def mean(x):
    return jnp.mean(x, axis=-1, keepdims=True)


def attn_fwd_kernel(len_ref,tok,w,b,cos,sin,qT,kT,vd,e,ctx,linv,Q2,KD,VA,S,flag,*,C,BQ,KC):
    iq=pl.program_id(1)
    length=len_ref[0,0]
    @pl.when(iq==0)
    def _():
        W=w[...].reshape(3*HD,w.shape[-1])
        p=dg(W,tok[...],1,1)+b[...].reshape(3*HD,1)
        c,s=cos[...],sin[...]
        def rot(x):
            u,v=x[:32],x[32:]
            return jnp.concatenate([u*c-v*s,v*c+u*s],axis=0)
        live=lax.broadcasted_iota(jnp.int32,(HD,C),1)<length
        q=rot(p[:HD]).astype(bf).astype(f32)
        k=jnp.where(live,rot(p[HD:2*HD]),0.0).astype(bf)
        v=jnp.where(live,p[2*HD:],0.0).astype(bf)
        qT[...]=(q*0.125).astype(bf)
        q=q*(0.125*LOG2E)
        hi=q.astype(bf)
        Q2[:HD,:]=hi
        Q2[HD:,:]=(q-hi.astype(f32)).astype(bf)
        kT[...]=k
        KD[...]=jnp.concatenate([k,k],axis=0).T
        vd[...]=jnp.concatenate([v,v],axis=0).T
        VA[:HD,:]=v
        VA[HD:,:]=jnp.where(live[:16],1.0,0.0).astype(bf)
        kf=k.astype(f32)
        qn=jnp.max(jnp.sum(q*q,axis=0,keepdims=True))
        kn=jnp.max(jnp.sum(kf*kf,axis=0,keepdims=True))
        flag[0]=(qn*kn<=1e4).astype(jnp.int32)
    cols=pl.ds(pl.multiple_of(iq*BQ,BQ),BQ)
    nk=C//KC
    def finish(o):
        inv=1.0/o[HD:HD+1]
        linv[...]=inv
        ctx[...]=(o[:HD]*inv).astype(bf)
    @pl.when(flag[0]==1)
    def _():
        qq=Q2[:,cols]
        for j in range(nk):
            r=slice(j*KC,(j+1)*KC)
            e[r,:]=jnp.exp2(dg(KD[r,:],qq,1,0)).astype(bf)
        finish(dg(VA[...],e[...],1,0))
    @pl.when(flag[0]==0)
    def _():
        qq=Q2[:,cols]
        keys=lax.broadcasted_iota(jnp.int32,(C,BQ),0)
        S[...]=jnp.where(keys<length,dg(KD[...],qq,1,0),-1e30)
        m=jnp.max(S[...],axis=0,keepdims=True)
        e[...]=jnp.exp2(S[...]-m).astype(bf)
        finish(dg(VA[...],e[...],1,0))
def attn_fwd(length,tok,w,b,cos,sin,*,BQ=None,KC=128):
    C,D=tok.shape; N,_,G=w.shape[:3]; H=N*G; BQ=BQ or C
    full=lambda h,i:(0,0)
    per=lambda h,i:(h,0,0)
    blk=lambda h,i:(h,0,i)
    grp=lambda h,i:(h//G,0,h%G,0,0)
    return pl.pallas_call(functools.partial(attn_fwd_kernel,C=C,BQ=BQ,KC=KC),
      grid=(H,C//BQ),
      in_specs=[pl.BlockSpec(memory_space=pltpu.SMEM),pl.BlockSpec((C,D),full),
        pl.BlockSpec((None,3,None,HD,D),grp),pl.BlockSpec((None,3,None,HD,1),grp),
        pl.BlockSpec((32,C),full),pl.BlockSpec((32,C),full)],
      out_specs=[pl.BlockSpec((None,HD,C),per),pl.BlockSpec((None,HD,C),per),pl.BlockSpec((None,C,128),per),
        pl.BlockSpec((None,C,BQ),blk),pl.BlockSpec((None,HD,BQ),blk),pl.BlockSpec((None,1,BQ),blk)],
      out_shape=[jax.ShapeDtypeStruct((H,HD,C),bf),jax.ShapeDtypeStruct((H,HD,C),bf),jax.ShapeDtypeStruct((H,C,128),bf),
        jax.ShapeDtypeStruct((H,C,C),bf),jax.ShapeDtypeStruct((H,HD,C),bf),jax.ShapeDtypeStruct((H,1,C),f32)],
      scratch_shapes=[pltpu.VMEM((128,C),bf),pltpu.VMEM((C,128),bf),pltpu.VMEM((80,C),bf),pltpu.VMEM((C,BQ),f32),pltpu.SMEM((1,),jnp.int32)],
      compiler_params=pltpu.CompilerParams(vmem_limit_bytes=60<<20),
      name="attn_fwd")(length,tok,w,b,cos,sin)


def ffn_kernel(tok,cot,ctxT,ow,up,dn,vec,ub,out,act,gu,hl_o,gl_o,g1_o,gol_o,dOT,sm,ubg,G,*,R):
    i=pl.program_id(0)
    @pl.when(i==0)
    def _():
        sm[...]=jnp.zeros_like(sm); ubg[...]=jnp.zeros_like(ubg)
    ob,g1,s1,db,g2,s2=[vec[k:k+1,:] for k in range(6)]
    D=tok.shape[1]; J=up.shape[0]
    def csum(k,x): sm[k:k+1,:]+=jnp.sum(x,axis=0,keepdims=True)
    W=ow[...]
    pre=tok[...].astype(f32)+dg(ctxT[...].reshape(D,R).T,W,1,0)+ob
    cen=pre-mean(pre)
    r1=lax.rsqrt(mean(cen*cen)+1e-6)
    n1=cen*r1
    hid=n1*g1+s1
    hl=hid.astype(bf)
    hl_o[...]=hl
    acc=hid+db
    F=up.shape[2]
    for j in range(J):
        u=dg(hl,up[j],1,0)+ub[j:j+1,:]
        phi=0.5*lax.erf(u*0.7071067811865476)+0.5
        a=(u*phi).astype(bf)
        act[:,j*F:(j+1)*F]=a
        G[:,j*F:(j+1)*F]=phi+u*(jnp.exp2(u*u*-0.7213475204444817)*0.3989422804014327)
        acc=acc+dg(a,dn[j],1,0)
    cen=acc-mean(acc)
    r2=lax.rsqrt(mean(cen*cen)+1e-6)
    n2=cen*r2
    out[...]=(n2*g2+s2).astype(bf)
    c=cot[...].astype(f32)
    csum(0,c*n2); csum(1,c)
    sg=c*g2
    gt=r2*(sg-mean(sg)-n2*mean(sg*n2))
    csum(2,gt)
    gl=gt.astype(bf)
    gl_o[...]=gl
    dh=gt
    for j in range(J):
        g=dg(gl,dn[j],1,1)*G[:,j*F:(j+1)*F]
        ubg[j:j+1,:]+=jnp.sum(g,axis=0,keepdims=True)
        gb=g.astype(bf)
        gu[:,j*F:(j+1)*F]=gb
        dh=dh+dg(gb,up[j],1,1)
    csum(3,dh*n1); csum(4,dh)
    sg=dh*g1
    go=r1*(sg-mean(sg)-n1*mean(sg*n1))
    csum(5,go)
    g1_o[...]=go
    gol=go.astype(bf)
    gol_o[...]=gol
    dOT[...]=dg(W,gol,1,1).astype(bf).reshape(dOT.shape)
def ffn(tok,cot,ctxT,ow,up,dn,vec,ub,*,R=512):
    C,D=tok.shape; J,_,F=up.shape; H,HD,_=ctxT.shape
    row=lambda w: pl.BlockSpec((R,w),lambda i:(i,0))
    fix=lambda a: pl.BlockSpec(a.shape,lambda i:(0,)*a.ndim,pipeline_mode=pl.Buffered(1))
    hb=pl.BlockSpec((H,HD,R),lambda i:(0,0,i))
    acc=lambda s: pl.BlockSpec(s,lambda i:(0,0))
    S=jax.ShapeDtypeStruct
    return pl.pallas_call(functools.partial(ffn_kernel,R=R),grid=(C//R,),
      in_specs=[row(D),row(D),hb,fix(ow),fix(up),fix(dn),fix(vec),fix(ub)],
      out_specs=[row(D),row(J*F),row(J*F),row(D),row(D),row(D),row(D),hb,acc((8,D)),acc((J,F))],
      out_shape=[S((C,D),bf),S((C,J*F),bf),S((C,J*F),bf),S((C,D),bf),S((C,D),bf),S((C,D),f32),S((C,D),bf),S((H,HD,C),bf),S((8,D),f32),S((J,F),f32)],
      scratch_shapes=[pltpu.VMEM((R,J*F),f32)],
      compiler_params=pltpu.CompilerParams(vmem_limit_bytes=63<<20),name="ffn")(tok,cot,ctxT,ow,up,dn,vec,ub)


def attn_bwd_kernel(len_ref,e,vd,dOT,ctxT,linv,qT,kT,cos,sin,gp,gb,D2,DI,DS,DST,ET,*,C,KC,var):
    length=len_ref[0,0]
    do=dOT[...].astype(f32)
    inv=linv[...]
    DI[...]=jnp.sum(do*ctxT[...].astype(f32),axis=0,keepdims=True)*inv
    do=do*inv
    hi=do.astype(bf)
    D2[:HD,:]=hi
    D2[HD:,:]=(do-hi.astype(f32)).astype(bf)
    nk=C//KC
    dk=[];dv=[];dq=None
    for j in range(nk):
        r=slice(j*KC,(j+1)*KC)
        dp=dg(vd[r,:],D2[...],1,0)
        ej=e[r,:]
        ds=(ej.astype(f32)*(dp-DI[...])).astype(bf)
        if var==1:
            DS[r,:]=ds
            DST[:,r]=ds.T
            ET[:,r]=ej.T
        else:
            dk.append(dg(qT[...],ds.T,1,0))
            dv.append(dg(D2[:HD,:],ej.T,1,0))
            q_=dg(kT[:,r],ds,1,0)
            dq=q_ if dq is None else dq+q_
    if var==1:
        dq=dg(kT[...],DS[...],1,0)
        dk=dg(qT[...],DST[...],1,0)
        dv=dg(D2[:HD,:],ET[...],1,0)
    else:
        dk=jnp.concatenate(dk,axis=1); dv=jnp.concatenate(dv,axis=1)
    live=lax.broadcasted_iota(jnp.int32,(HD,C),1)<length
    c,s=cos[...],sin[...]
    def unrot(x):
        u,w=x[:32],x[32:]
        return jnp.concatenate([u*c+w*s,w*c-u*s],axis=0)
    def put(k,x):
        gp[k]=x.astype(bf)
        gb[k]=jnp.sum(x,axis=1,keepdims=True)
    put(0,unrot(dq*0.125))
    put(1,unrot(jnp.where(live,dk,0.0)))
    put(2,jnp.where(live,dv,0.0))
def attn_bwd(length,e,vd,dOT,ctxT,linv,qT,kT,cos,sin,*,KC=256,var=1,G=3):
    H,C,_=e.shape
    per=lambda h:(h,0,0)
    hb=pl.BlockSpec((None,HD,C),per)
    tab=pl.BlockSpec((32,C),lambda h:(0,0))
    grp=lambda h:(h//G,0,h%G,0,0)
    return pl.pallas_call(functools.partial(attn_bwd_kernel,C=C,KC=KC,var=var),grid=(H,),
      in_specs=[pl.BlockSpec(memory_space=pltpu.SMEM),pl.BlockSpec((None,C,C),per),pl.BlockSpec((None,C,128),per),hb,hb,pl.BlockSpec((None,1,C),per),hb,hb,tab,tab],
      out_specs=[pl.BlockSpec((None,3,None,HD,C),grp),pl.BlockSpec((None,3,None,HD,1),grp)],
      out_shape=[jax.ShapeDtypeStruct((H//G,3,G,HD,C),bf),jax.ShapeDtypeStruct((H//G,3,G,HD,1),f32)],
      scratch_shapes=[pltpu.VMEM((128,C),bf),pltpu.VMEM((1,C),f32)]+[pltpu.VMEM((C,C),bf)]*3,
      compiler_params=pltpu.CompilerParams(vmem_limit_bytes=63<<20),name="attn_bwd")(length,e,vd,dOT,ctxT,linv,qT,kT,cos,sin)


def rotary_tables(capacity):
    positions = jnp.arange(capacity).astype(f32)
    frequencies = 10000.0 ** (-2.0 * jnp.arange(HD // 2).astype(f32) / HD)
    angles = frequencies[:, None] * positions[None, :]
    return jnp.cos(angles), jnp.sin(angles)


def gather_all(local):
    wide, narrow = lax.axis_size("wide"), lax.axis_size("narrow")
    rows = local.shape[0] // wide
    piece = lax.dynamic_slice_in_dim(local, lax.axis_index("wide") * rows, rows, 0)
    full = lax.all_gather(piece, ("narrow", "wide"), axis=0, tiled=True)
    return full.reshape((narrow,) + local.shape)


def reduce_all(full):
    part = lax.psum_scatter(full.astype(bf), "wide", scatter_dimension=1, tiled=True)
    part = lax.psum_scatter(part, "narrow", scatter_dimension=0, tiled=True)
    return lax.all_gather(part[0], "wide", axis=0, tiled=True).astype(f32)


def shards(
    tokens, lengths, qkv_weight, qkv_bias, out_weight, out_bias, norm1_gain, norm1_shift,
    up_weight, up_bias, down_weight, down_bias, norm2_gain, norm2_shift, cotangent,
):
    narrow = lax.axis_size("narrow")
    me = lax.axis_index("narrow")
    tok, cot = tokens[0], cotangent[0]
    capacity, width = tok.shape
    heads_here = HEADS // narrow
    length = lax.dynamic_slice(lengths, (0, me), (1, 1))
    cos, sin = rotary_tables(capacity)
    qkv_t = qkv_weight.transpose(1, 2, 0).reshape(3 * heads_here * HD, width)
    wq = gather_all(qkv_t).reshape(narrow, 3, heads_here, HD, width)
    ow = gather_all(out_weight).reshape(HEADS * HD, width)
    up = gather_all(up_weight)
    dn = gather_all(down_weight)
    biases = lax.all_gather(jnp.concatenate([qkv_bias.reshape(-1), up_bias]), "narrow").astype(f32)
    n_qkv = qkv_bias.size
    bq = biases[:, :n_qkv].reshape(narrow, 3, heads_here, HD, 1)
    ub = biases[:, n_qkv:]
    vec = jnp.stack([out_bias, norm1_gain, norm1_shift, down_bias, norm2_gain, norm2_shift]).astype(f32)
    q_t, k_t, v_d, e, ctx_t, linv = attn_fwd(length, tok, wq, bq, cos, sin)
    out, act, gu, hid, g2, g1, g1_low, do_t, small, ub_grad = ffn(tok, cot, ctx_t, ow, up, dn, vec, ub)
    hidden = act.shape[1] // narrow
    dn_grad = dg(act, g2, 0, 0).reshape(narrow, hidden, width)
    up_grad = jnp.stack([dg(hid, gu[:, j * hidden:(j + 1) * hidden], 0, 0) for j in range(narrow)])
    ow_grad = dg(ctx_t.reshape(HEADS * HD, capacity), g1_low, 1, 0).reshape(narrow, heads_here * HD, width)
    gp, gb = attn_bwd(length, e, v_d, do_t, ctx_t, linv, q_t, k_t, cos, sin, G=heads_here)
    gp = gp.reshape(-1, capacity)
    qkv_grad = dg(gp, tok, 1, 0).reshape((narrow,) + qkv_t.shape)
    input_grad = dg(gp, wq.reshape(-1, width), 0, 0) + g1
    packed = jnp.concatenate([small[:6].reshape(-1), ub_grad.reshape(-1), gb.reshape(-1)])
    packed = lax.psum(packed, ("wide", "narrow"))
    small = packed[:6 * width].reshape(6, width)
    ub_grad = lax.dynamic_index_in_dim(packed[6 * width:6 * width + ub_grad.size].reshape(narrow, -1), me, 0, False)
    gb = lax.dynamic_index_in_dim(packed[6 * width + narrow * hidden:].reshape(narrow, 3, -1), me, 0, False)
    dn_grad, up_grad, ow_grad, qkv_grad = [reduce_all(x) for x in (dn_grad, up_grad, ow_grad, qkv_grad)]
    qkv_grad = qkv_grad.reshape(3, heads_here * HD, width).transpose(2, 0, 1)
    return (
        out[None], input_grad[None], qkv_grad, gb, ow_grad, small[5], small[3], small[4],
        up_grad, ub_grad, dn_grad, small[2], small[0], small[1],
    )


def solution(mesh):
    rows = P(("wide", "narrow"), None, None)
    weights = (P(None, None, "narrow"), P(None, "narrow"), P("narrow", None), P(), P(), P(),
               P(None, "narrow"), P("narrow"), P("narrow", None), P(), P(), P())
    return jax.shard_map(
        shards, mesh=mesh, in_specs=(rows, P("wide", None)) + weights + (rows,),
        out_specs=(rows, rows) + weights, check_vma=False,
    )
```

time: 2790 us -> 687 us (0.25)
  waiting for transfers between devices: 1780 us -> 327 us
  matrix products: 459 us -> 48.1 us
  other arithmetic: 266 us -> 13.7 us
  Pallas kernels: 0 us -> 159 us
  local copies, waits for them, and re-layouts: 157 us -> 33.6 us
  loops' own time: 49.4 us -> 0 us
  blocking collectives: 42.9 us -> 81.6 us
    reduce_scatter x4 -> x6, waiting for transfers between devices: 993 us -> 63.9 us  [the longest x4 44.7 us: reduce_all(): part = lax.psum_scatter(part, 'narrow', scatter_dimension=0, tiled=True)]
    all_gather x4 -> x6, waiting for transfers between devices: 671 us -> 172 us  [the longest x4 159 us: gather_all(): full = lax.all_gather(piece, ('narrow', 'wide'), axis=0, tiled=True)]
    dot_general x96 -> x8, matrix products: 459 us -> 48.1 us  [dg(): lax.dot_general(a, b, (((ca,), (cb,)), ((), ())), preferred_element_type=...]
    pallas_call x0 -> x3, Pallas kernels: none -> 159 us  [the longest x1 55.1 us: attn_fwd(): pl.pallas_call(functools.partial(attn_fwd_kernel, C=C, BQ=BQ, KC=KC), gri...]
    convert_element_type x25 -> x5, other arithmetic: 165 us -> 7.23 us  [the longest x3 6.62 us: reduce_all(): return lax.all_gather(part[0], 'wide', axis=0, tiled=True).astype(f32)]
    psum x1 -> x0, waiting for transfers between devices: 114 us -> none  [shards(): lax.psum((qkv_grad, qkv_bias_grad, out_grad, small_grads[4], small_grads[...]
    unnamed x9 -> x16, waiting for transfers between devices: 0.81 us -> 91.4 us
    reduce_sum x21 -> x0, other arithmetic: 58.1 us -> none  [the longest x12 25 us: one_block(): denominator = jnp.sum(exponentials, axis=-1, keepdims=True)]
  transfers between devices with their start and end apart: 9 -> 14, of which waited for: 9 -> 10; matrix products, arithmetic and copies ran while one was open for 2% -> 11% of each run, Pallas kernels for 0% -> 16%
where the time goes in v1:
time: 687 us; the launch traced here: 679 us
  waiting for transfers between devices  327 us (48%)
  Pallas kernels  159 us (23%)
  blocking collectives  81.6 us (12%)
  matrix products  48.1 us (7%)
  local copies, waits for them, and re-layouts  33.6 us (5%)
  between operations  15.3 us (2%)
  other arithmetic  13.7 us (2%)
    all_gather x4, waiting for transfers between devices, gather_all(): full = lax.all_gather(piece, ('narrow', 'wide'), axis=0, tiled=True)  159 us
    unnamed x16, waiting for transfers between devices  91.4 us
    pallas_call x1, Pallas kernels, attn_fwd(): pl.pallas_call(functools.partial(attn_fwd_kernel, C=C, BQ=BQ, KC=KC), gri...  55.1 us
    pallas_call x1, Pallas kernels, attn_bwd(): pl.pallas_call(functools.partial(attn_bwd_kernel, C=C, KC=KC, var=var), g...  53.7 us
    pallas_call x1, Pallas kernels, ffn(): pl.pallas_call(functools.partial(ffn_kernel, R=R), grid=(C // R,), in_spe...  50.5 us
    dot_general x8, matrix products, dg(): lax.dot_general(a, b, (((ca,), (cb,)), ((), ())), preferred_element_type=...  48.1 us
    reduce_scatter x4, waiting for transfers between devices, reduce_all(): part = lax.psum_scatter(part, 'narrow', scatter_dimension=0, tiled=True)  44.7 us
    psum x1, blocking collectives, shards(): packed = lax.psum(packed, ('wide', 'narrow'))  39.6 us
  transfers between devices with their start and end apart: 14, of which 10 were waited for; matrix products, arithmetic and copies ran while one was open for 11% of the time, Pallas kernels for 16%

profile of v1, /device:TPU:0, one launch (start us, length us, event | category | flops | bytes accessed | tf_op | source)
XLA Modules:
  0.0 679.4 jit_solution(1862418734475818066)
XLA Ops:
  7.3 1.1 copy-done
  8.4 0.7 constant_dynamic-slice_fusion.3
  9.1 1.4 constant_dynamic-slice_fusion.2
  10.5 1.6 constant_dynamic-slice_fusion.1
  12.2 1.6 constant_dynamic-slice_fusion
  13.9 0.8 reshape.104
  14.6 1.2 dynamic-slice
  16.5 0.8 pad_maximum_fusion.2
  17.5 20.5 %all-reduce = bf16[5376]{0:T(1024)(128)(2,1)S(1)} all-reduce(bf16[5376]{0:T(1024)(128)(2,1)S(1)} %dynamic-update-slice), channel_id=2, replica_groups=mesh['wide'=8,'narrow'=4] {'narrow'}, use_global_device_ids=true, to_apply=%add | all-reduce | flops 5376 | bytes 21504
  38.1 0.7 slice.85.ub
  38.8 0.7 stack.41
  39.5 0.7 stack.42
  40.1 0.7 stack.43
  40.8 0.7 stack.44
  41.5 0.7 stack.45
  42.2 0.7 stack.46
  42.9 0.6 convert_element_type.58.vec
  43.5 2.0 reshape.133.b
  45.6 0.6 constant_dynamic-slice_fusion.4.len_ref
  46.2 1.5 multiply_sine_fusion
  47.7 26.7 %all-gather.12.cloned.1.call-done = bf16[2304,768]{1,0:T(8,128)(2,1)} async-done(((bf16[72,768]{1,0:T(8,128)(2,1)}), bf16[2304,768]{1,0:T(8,128)(2,1)}) %all-gather.12.cloned.1.call-update) | async-done | bytes 3538960 | tf_op jit(solution)/shard_map/all_gather | solution.py:227
  74.4 55.1 %attn_fwd.1 = (bf16[12,64,1536]{2,1,0:T(8,128)(2,1)}, bf16[12,64,1536]{2,1,0:T(8,128)(2,1)}, bf16[12,1536,128]{2,1,0:T(8,128)(2,1)}, bf16[12,1536,1536]{2,1,0:T(...) custom-call(s32[1,1]{1,0:T(1,128)} %constant_dynamic-slice_fusion.4.len_ref, ...), custom_call_target="tpu_custom_call" | custom-call | tf_op jit(solution)/shard_map/attn_fwd/pallas_call | solution.py:80
  129.5 0.7 all-gather.14.cloned.1.call-done.ow
  130.2 66.1 %all-gather.16.cloned.1.call-done = bf16[3072,768]{1,0:T(8,128)(2,1)} async-done(((bf16[96,768]{1,0:T(8,128)(2,1)}), bf16[3072,768]{1,0:T(8,128)(2,1)}) %all-gather.16.cloned.1.call-update) | async-done | bytes 4718608 | tf_op jit(solution)/shard_map/all_gather | solution.py:227
  196.2 65.2 %all-gather.18.cloned.1.call-done = bf16[3072,768]{1,0:T(8,128)(2,1)} async-done(((bf16[96,768]{1,0:T(8,128)(2,1)}), bf16[3072,768]{1,0:T(8,128)(2,1)}) %all-gather.18.cloned.1.call-update) | async-done | bytes 4718608 | tf_op jit(solution)/shard_map/all_gather | solution.py:227
  261.5 50.5 %ffn.1 = (bf16[1536,768]{1,0:T(8,128)(2,1)}, bf16[1536,3072]{1,0:T(8,128)(2,1)}, bf16[1536,3072]{1,0:T(8,128)(2,1)}, bf16[1536,768]{1,0:T(8,128)(2,1)}, bf16[153...) custom-call(bf16[1536,768]{1,0:T(8,128)(2,1)} %bitcast.71, ...), custom_call_target="tpu_custom_call" | custom-call | tf_op jit(solution)/shard_map/ffn/pallas_call | solution.py:152
  312.0 4.6 fusion.26
  317.1 0.7 copy-done.8
  317.8 2.1 fusion.29
  319.9 2.1 fusion.32
  322.0 2.1 fusion.35
  324.1 2.4 pad_maximum_fusion
  326.6 1.6 copy-done.7
  328.2 13.7 %convolution_convert_fusion = bf16[3072,768]{1,0:T(8,128)(2,1)} fusion(bf16[1536,3072]{1,0:T(8,128)(2,1)} %get-tuple-element.48, bf16[1536,768]{1,0:T(8,128)(2,1)S(1)} %copy-done.7), kind=kOutput, calls=%fused_computation | convolution fusion | flops 7250116608 | bytes 16515072 | tf_op jit(solution)/shard_map/dot_general | solution.py:17
  342.1 1.4 copy-done.2
  343.5 3.6 fusion.23
  347.2 0.9 copy.34
  348.1 1.2 copy.37
  349.4 53.7 %attn_bwd.1 = (bf16[4,3,3,64,1536]{4,3,2,1,0:T(8,128)(2,1)}, f32[4,3,3,64,1]{4,3,2,1,0:T(8,128)}) custom-call(s32[1,1]{1,0:T(1,128)} %constant_dynamic-slice_fusion.4.len_ref, bf16[12,1536,1536]{2,1,0:T(8,128)(2,1)} %get-tuple-element.34.e, bf16[12,1536,128]{2,1,0:T(8,128)(2,1)} %get-tuple-element.35.vd, bf16[12,64,1536]{2,1,0:T(8,128)(2,1)} %get-tuple-element.36.dOT, ...), custom_call_target="tpu_custom_call" | custom-call | tf_op jit(solution)/shard_map/attn_bwd/pallas_call | solution.py:208
  403.1 8.6 %convolution_convert_fusion.1 = bf16[4,576,768]{2,1,0:T(8,128)(2,1)S(1)} fusion(bf16[4,576,1536]{2,1,0:T(8,128)(2,1)} %bitcast.83, bf16[1,1536,768]{2,1,0:T(8,128)(2,1)} %param.15), kind=kOutput, calls=%fused_computation.3 | convolution fusion | flops 5437587456 | bytes 12976128 | tf_op jit(solution)/shard_map/dot_general | solution.py:17
  411.7 2.7 copy.32
  414.5 2.6 copy.36
  417.1 0.7 reduce-scatter.19.cloned.1.call-update
  417.8 19.2 %reduce-scatter.21.cloned.1.call-done = bf16[4,96,768]{2,1,0:T(8,128)(2,1)} async-done(((bf16[4,768,768]{2,1,0:T(8,128)(2,1)}), bf16[4,96,768]{2,1,0:T(8,128)(2,1)}) %reduce-scatter.21.cloned.1.call-update) | async-done | bytes 589840 | tf_op jit(solution)/shard_map/reduce_scatter | solution.py:232
  437.4 39.7 %reduce-scatter.27.cloned.1.call-done = bf16[24,3072]{1,0:T(8,128)(2,1)} async-done(((bf16[192,3072]{1,0:T(8,128)(2,1)}), bf16[24,3072]{1,0:T(8,128)(2,1)}) %reduce-scatter.27.cloned.1.call-update) | async-done | bytes 147472
  477.1 1.0 reshape.137
  478.1 0.7 copy.35
  478.8 50.8 %reduce-scatter.25.cloned.1.call-done = bf16[72,3072]{1,0:T(8,128)(2,1)} async-done(((bf16[576,3072]{1,0:T(8,128)(2,1)}), bf16[72,3072]{1,0:T(8,128)(2,1)}) %reduce-scatter.25.cloned.1.call-update) | async-done | bytes 442384
  529.6 1.3 reshape.135
  531.0 0.8 copy.33
  531.9 22.2 %reduce-scatter.19.cloned.1.call-done = bf16[1,96,768]{2,1,0:T(8,128)(2,1)} async-done(((bf16[4,96,768]{2,1,0:T(8,128)(2,1)}), bf16[1,96,768]{2,1,0:T(8,128)(2,1)}) %reduce-scatter.19.cloned.1.call-update) | async-done | bytes 147472 | tf_op jit(solution)/shard_map/reduce_scatter | solution.py:233
  554.1 22.5 %reduce-scatter.23.cloned.1.call-done = bf16[1,96,768]{2,1,0:T(8,128)(2,1)} async-done(((bf16[4,96,768]{2,1,0:T(8,128)(2,1)}), bf16[1,96,768]{2,1,0:T(8,128)(2,1)}) %reduce-scatter.23.cloned.1.call-update) | async-done | bytes 147472 | tf_op jit(solution)/shard_map/reduce_scatter | solution.py:233
  576.7 11.2 %add_bitcast_fusion = f32[1,1536,768]{2,1,0:T(8,128)} fusion(f32[1536,768]{1,0:T(8,128)} %get-tuple-element.41, bf16[2304,1536]{1,0:T(8,128)(2,1)} %bitcast.84, bf16[2304,768]{1,0:T(8,128)(2,1)} %all-gather.12.cloned.1.call-done), kind=kOutput, calls=%fused_computation.2 | convolution fusion | flops 5436997632 | bytes 20054016 | tf_op jit(solution)/shard_map/dot_general | solution.py:17
  588.4 39.6 %psum.7 = f32[9984]{0:T(1024)S(1)} all-reduce(f32[9984]{0:T(1024)S(1)} %pad_maximum_fusion.1), channel_id=1, replica_groups=mesh['wide'=8,'narrow'=4] {'wide','narrow'}, use_global_device_ids=true, to_apply=%region_2.3 | all-reduce | flops 9984 | bytes 79872 | tf_op jit(solution)/shard_map/psum | solution.py:269
  628.1 0.6 dynamic-slice_reduce_fusion
  628.8 0.6 dynamic-slice_bitcast_fusion
  629.3 0.6 fusion.38
  630.0 11.0 %all-gather.2 = bf16[1,192,768]{2,1,0:T(8,128)(2,1)S(1)} all-gather(bf16[1,24,768]{2,1,0:T(8,128)(2,1)} %reduce-scatter.15.cloned.1.call-done), channel_id=4, replica_groups=mesh['wide'=8,'narrow'=4] {'wide'}, dimensions={1}, use_global_device_ids=true | all-gather | bytes 331776 | tf_op jit(solution)/shard_map/all_gather | solution.py:234
  640.9 0.9 bitcast_convert_fusion.2
  641.8 10.6 %all-gather.1 = bf16[1,576,768]{2,1,0:T(8,128)(2,1)S(1)} all-gather(bf16[1,72,768]{2,1,0:T(8,128)(2,1)} %reduce-scatter.13.cloned.1.call-done), channel_id=3, replica_groups=mesh['wide'=8,'narrow'=4] {'wide'}, dimensions={1}, use_global_device_ids=true | all-gather | bytes 995328 | tf_op jit(solution)/shard_map/all_gather | solution.py:234
  652.4 1.3 convert_bitcast_fusion
  653.7 2.9 bitcast_convert_fusion.1
  656.6 13.0 %all-gather.22.cloned.1.call-done = bf16[1,768,768]{2,1,0:T(8,128)(2,1)} async-done(((bf16[1,96,768]{2,1,0:T(8,128)(2,1)}), bf16[1,768,768]{2,1,0:T(8,128)(2,1)}) %all-gather.22.cloned.1.call-update) | async-done | bytes 1179664 | tf_op jit(solution)/shard_map/all_gather | solution.py:234
  669.6 2.8 bitcast_convert_fusion
  (63 shorter events, 2.8 us)
Async XLA Ops:
  7.2 1.2 copy-start
  7.2 38.4 %copy-start.9 = (s32[1,4]{1,0:T(1,128)S(1)}, s32[1,4]{1,0:T(1,128)}, u32[]{:S(2)}) copy-start(s32[1,4]{1,0:T(1,128)} %param.16) | copy-start | bytes 52
  7.2 67.2 %all-gather.12.cloned.1.call-start = ((), (), s32[]{:S(2)}) async-start(), calls=%async_computation.8 | async-start | bytes 3649536 | tf_op jit(solution)/shard_map/all_gather | solution.py:227
  9.0 121.1 %all-gather.14.cloned.1.call-start = ((), (), s32[]{:S(2)}) async-start(), calls=%async_computation.9 | async-start | bytes 1216512 | tf_op jit(solution)/shard_map/all_gather | solution.py:227
  10.5 185.8 %all-gather.16.cloned.1.call-start = ((), (), s32[]{:S(2)}) async-start(), calls=%async_computation.10 | async-start | bytes 4866048 | tf_op jit(solution)/shard_map/all_gather | solution.py:227
  12.2 249.3 %all-gather.18.cloned.1.call-start = ((), (), s32[]{:S(2)}) async-start(), calls=%async_computation.11 | async-start | bytes 4866048 | tf_op jit(solution)/shard_map/all_gather | solution.py:227
  13.8 403.3 %reduce-scatter.17.cloned.1.call-start = ((), (), s32[]{:S(2)}) async-start(), calls=%async_computation.14 | async-start | bytes 5308416 | tf_op jit(solution)/shard_map/reduce_scatter | solution.py:232
  312.0 5.1 copy-start.6
  312.0 5.8 copy-start.8
  326.5 1.7 copy-start.7
  326.5 110.5 %reduce-scatter.21.cloned.1.call-start = ((), (), s32[]{:S(2)}) async-start(), calls=%async_computation.16 | async-start | bytes 5308416 | tf_op jit(solution)/shard_map/reduce_scatter | solution.py:232
  341.8 1.7 copy-start.2
  341.9 135.2 %reduce-scatter.27.cloned.1.call-start = ((), (), s32[]{:S(2)}) async-start(), calls=%async_computation.21 | async-start | bytes 1327104
  349.4 180.3 %reduce-scatter.25.cloned.1.call-start = ((), (), s32[]{:S(2)}) async-start(), calls=%async_computation.20 | async-start | bytes 3981312
  417.0 137.0 %reduce-scatter.19.cloned.1.call-start = ((), (), s32[]{:S(2)}) async-start(), calls=%async_computation.15 | async-start | bytes 737280 | tf_op jit(solution)/shard_map/reduce_scatter | solution.py:233
  417.8 158.8 %reduce-scatter.23.cloned.1.call-start = ((), (), s32[]{:S(2)}) async-start(), calls=%async_computation.17 | async-start | bytes 737280 | tf_op jit(solution)/shard_map/reduce_scatter | solution.py:233
  437.1 192.9 %reduce-scatter.15.cloned.1.call-start = ((), (), s32[]{:S(2)}) async-start(), calls=%async_computation.13 | async-start | bytes 184320 | tf_op jit(solution)/shard_map/reduce_scatter | solution.py:233
  478.8 163.0 %reduce-scatter.13.cloned.1.call-start = ((), (), s32[]{:S(2)}) async-start(), calls=%async_computation.12 | async-start | bytes 552960 | tf_op jit(solution)/shard_map/reduce_scatter | solution.py:233
  531.8 121.9 %all-gather.20.cloned.1.call-start = ((), (), s32[]{:S(2)}) async-start(), calls=%async_computation.18 | async-start | bytes 1327104 | tf_op jit(solution)/shard_map/all_gather | solution.py:234
  554.1 115.5 %all-gather.22.cloned.1.call-start = ((), (), s32[]{:S(2)}) async-start(), calls=%async_computation.19 | async-start | bytes 1327104 | tf_op jit(solution)/shard_map/all_gather | solution.py:234
  576.6 11.3 %copy-start.3 = (f32[4,3,3,64,1]{4,3,2,1,0:T(8,128)S(1)}, f32[4,3,3,64,1]{4,3,2,1,0:T(8,128)}, u32[]{:S(2)}) copy-start(f32[4,3,3,64,1]{4,3,2,1,0:T(8,128)} %get-tuple-element.44) | copy-start | bytes 27652
  576.6 11.8 %copy-start.5 = (f32[4,768]{1,0:T(4,128)S(1)}, f32[4,768]{1,0:T(4,128)}, u32[]{:S(2)}) copy-start(f32[4,768]{1,0:T(4,128)} %get-tuple-element.43) | copy-start | bytes 36868
  576.6 11.8 %copy-start.4 = (f32[8,768]{1,0:T(8,128)S(1)}, f32[8,768]{1,0:T(8,128)}, u32[]{:S(2)}) copy-start(f32[8,768]{1,0:T(8,128)} %get-tuple-element.42) | copy-start | bytes 73732
  653.7 18.7 %copy-start.1 = (bf16[768,3,192]{0,2,1:T(8,128)(2,1)S(1)}, bf16[768,3,192]{0,2,1:T(8,128)(2,1)}, u32[]{:S(2)}) copy-start(bf16[768,3,192]{0,2,1:T(8,128)(2,1)} %param.17) | copy-start | bytes 2654212
Sparse Core Ops, SparseCore 0:
  11.5 62.8 all-gather.11
  77.3 52.8 all-gather.13
  133.7 62.5 all-gather.15
  199.0 62.4 all-gather.17
  326.7 52.7 reduce-scatter.16
  383.1 53.8 reduce-scatter.20
  440.3 36.7 reduce-scatter.26
  481.5 48.0 reduce-scatter.24
  532.0 21.9 reduce-scatter.18
  556.3 20.2 reduce-scatter.22
  579.5 17.5 reduce-scatter.14
  599.9 19.3 reduce-scatter.12
  621.3 22.6 all-gather.19
  645.9 23.6 all-gather.21

commit v2 on v1

v2 whole, which is shorter than its diff:
```python
import functools

import jax
import jax.numpy as jnp
from jax import lax
from jax.experimental import pallas as pl
from jax.experimental.pallas import tpu as pltpu
from jax.sharding import PartitionSpec as P

bf = jnp.bfloat16
f32 = jnp.float32
LOG2E = 1.4426950408889634
HEADS = 12
HD = 64
SPLIT = 8
EXTRA = 8
MIB = 1 << 20


def dg(a, b, ca, cb):
    return lax.dot_general(a, b, (((ca,), (cb,)), ((), ())), preferred_element_type=f32)


def mean(x):
    return jnp.mean(x, axis=-1, keepdims=True)


def shape(s, d):
    return jax.ShapeDtypeStruct(s, d)


SMEM = pl.BlockSpec(memory_space=pltpu.SMEM)
ANY = pl.BlockSpec(memory_space=pl.ANY)


def params(mib):
    return pltpu.CompilerParams(vmem_limit_bytes=mib * MIB)


def cost(flops, nbytes):
    return pl.CostEstimate(flops=1, bytes_accessed=1, transcendentals=0)


def put_piece(meta, src, g, lanes, place, dst, sem):
    rel, half, whole = place
    rows = src.shape[1]
    at = 0 if rel is None else (meta[0, 1] ^ rel) * whole + half
    return pltpu.make_async_copy(src.at[g, :, lanes], dst.at[pl.ds(pl.multiple_of(at, 16), rows), :], sem)


def attn_fwd_kernel(meta, *refs, C, KC, G, layout, own):
    pieces, refs = refs[:len(layout)], refs[len(layout):]
    x, b, cos, sin, q_t, k_t, v_d, e, ctx, linv, w_t, *rest = refs
    if own:
        x_t, Q2, KD, VA, S, W, flag, sem = rest
    else:
        x_t, (Q2, KD, VA, S, W, flag, sem) = x, rest
    h = pl.program_id(0)
    length = meta[0, 0]
    groups = pieces[0].shape[0]

    def copies(g):
        return [put_piece(meta, pieces[t], g, slice(None), layout[t], W.at[g], sem.at[g, t]) for t in range(len(pieces))]

    @pl.when(h == 0)
    def _():
        for g in range(groups):
            for c in copies(g):
                c.start()
        if own:
            x_t[...] = x[...].T

    for g in range(groups):
        @pl.when(h == g * G)
        def _(g=g):
            for c in copies(g):
                c.wait()
            w_t[...] = W[g].T

    at = lax.rem(h, G)
    w = jnp.concatenate([w_t[pl.ds(pl.multiple_of((p * G + at) * HD, HD), HD), :] for p in range(3)], axis=0)
    p = dg(w, x_t[...], 1, 0) + b[...].reshape(3 * HD, 1)
    c, s = cos[...], sin[...]

    def rot(v):
        u, z = v[:HD // 2], v[HD // 2:]
        return jnp.concatenate([u * c - z * s, z * c + u * s], axis=0)

    live = lax.broadcasted_iota(jnp.int32, (HD, C), 1) < length
    q = rot(p[:HD]).astype(bf).astype(f32)
    k = jnp.where(live, rot(p[HD:2 * HD]), 0.0).astype(bf)
    v = jnp.where(live, p[2 * HD:], 0.0).astype(bf)
    q_t[...] = (q * 0.125).astype(bf)
    q = q * (0.125 * LOG2E)
    hi = q.astype(bf)
    Q2[:HD, :] = hi
    Q2[HD:, :] = (q - hi.astype(f32)).astype(bf)
    k_t[...] = k
    KD[...] = jnp.concatenate([k, k], axis=0).T
    v_d[...] = jnp.concatenate([v, v], axis=0).T
    VA[:HD, :] = v
    VA[HD:, :] = jnp.where(live[:16], 1.0, 0.0).astype(bf)
    kf = k.astype(f32)
    qn = jnp.max(jnp.sum(q * q, axis=0, keepdims=True))
    kn = jnp.max(jnp.sum(kf * kf, axis=0, keepdims=True))
    flag[0] = (qn * kn <= 1e4).astype(jnp.int32)

    @pl.when(flag[0] == 1)
    def _():
        for j in range(C // KC):
            r = slice(j * KC, (j + 1) * KC)
            e[r, :] = jnp.exp2(dg(KD[r, :], Q2[...], 1, 0)).astype(bf)

    @pl.when(flag[0] == 0)
    def _():
        BQ = S.shape[1]

        def block(i, carry):
            cols = pl.ds(pl.multiple_of(i * BQ, BQ), BQ)
            keys = lax.broadcasted_iota(jnp.int32, (C, BQ), 0)
            S[...] = jnp.where(keys < length, dg(KD[...], Q2[:, cols], 1, 0), -1e30)
            m = jnp.max(S[...], axis=0, keepdims=True)
            e[:, cols] = jnp.exp2(S[...] - m).astype(bf)
            return carry

        lax.fori_loop(0, C // BQ, block, 0)

    o = dg(VA[...], e[...], 1, 0)
    inv = 1.0 / o[HD:HD + 1]
    linv[...] = inv
    ctx[...] = (o[:HD] * inv).astype(bf)


def attn_fwd(meta, pieces, layout, x, b, cos, sin, own):
    groups, _, D = pieces[0].shape
    C = x.shape[0] if own else x.shape[1]
    G = b.shape[2]
    H = groups * G
    per = lambda h: (h, 0, 0)
    fix = lambda a: pl.BlockSpec(a.shape, lambda h: (0,) * a.ndim, pipeline_mode=pl.Buffered(1))
    hb = pl.BlockSpec((None, HD, C), per)
    out_specs = [hb, hb, pl.BlockSpec((None, C, 2 * HD), per), pl.BlockSpec((None, C, C), per), hb,
                 pl.BlockSpec((None, 1, C), per), pl.BlockSpec((None, D, D), lambda h: (h // G, 0, 0))]
    out_shape = [shape((H, HD, C), bf), shape((H, HD, C), bf), shape((H, C, 2 * HD), bf), shape((H, C, C), bf),
                 shape((H, HD, C), bf), shape((H, 1, C), f32), shape((groups, D, D), bf)]
    if own:
        out_specs.append(pl.BlockSpec((D, C), lambda h: (0, 0)))
        out_shape.append(shape((D, C), bf))
    return pl.pallas_call(
        functools.partial(attn_fwd_kernel, C=C, KC=min(128, C), G=G, layout=layout, own=own), grid=(H,),
        in_specs=[SMEM] + [ANY] * len(pieces) + [fix(x), pl.BlockSpec((None, 3, None, HD, 1), lambda h: (h // G, 0, h % G, 0, 0)), fix(cos), fix(sin)],
        out_specs=out_specs, out_shape=out_shape,
        scratch_shapes=[pltpu.VMEM((2 * HD, C), bf), pltpu.VMEM((C, 2 * HD), bf), pltpu.VMEM((HD + 16, C), bf),
                        pltpu.VMEM((C, C // 3 if C % 384 == 0 else C), f32), pltpu.VMEM((groups, D, D), bf), pltpu.SMEM((1,), jnp.int32),
                        pltpu.SemaphoreType.DMA((groups, len(pieces)))],
        compiler_params=params(60), cost_estimate=cost(H * (4 * C * C * 256 + 2 * C * D * 3 * HD), H * C * C * 2 + 8 * MIB),
        name="attn_fwd_own" if own else "attn_fwd",
    )(meta, *pieces, x, b, cos, sin)


def ffn_kernel(meta, u_own, d_own, *refs, R, layout):
    pieces, refs = refs[:len(layout)], refs[len(layout):]
    tok, cot, *refs = refs
    J = pieces[0].shape[0] + 1
    ctxs, ows, refs = refs[:2], refs[2:4], refs[4:]
    (vec, ub, out, act, gu, hid_t, gl_t, g1_o, gol_t, do_t, small, ubg, G, U, Dn, sem) = refs
    i = pl.program_id(0)
    groups = J - 1

    def copies():
        cs = [pltpu.make_async_copy(u_own, U.at[0], sem.at[0, 0, 0]), pltpu.make_async_copy(d_own, Dn.at[0], sem.at[1, 0, 0])]
        for g in range(groups):
            for t, (piece, (parts, place)) in enumerate(zip(pieces, layout)):
                for k, s in enumerate(parts):
                    lanes = slice(k * U.shape[2], (k + 1) * U.shape[2])
                    cs.append(put_piece(meta, piece, g, lanes, place, (U, Dn)[s].at[g + 1], sem.at[s, g + 1, t]))
        return cs

    @pl.when(i == 0)
    def _():
        for c in copies():
            c.start()
        small[...] = jnp.zeros_like(small)
        ubg[...] = jnp.zeros_like(ubg)
        for c in copies():
            c.wait()

    ob, g1, s1, db, g2, s2 = [vec[k:k + 1, :] for k in range(6)]
    D = tok.shape[1]
    F = U.shape[2]

    def csum(k, x):
        small[k:k + 1, :] += jnp.sum(x, axis=0, keepdims=True)

    ow = jnp.concatenate([w[g] for w in ows for g in range(w.shape[0])], axis=0)
    ctx = jnp.concatenate([c[...].reshape(-1, R) for c in ctxs], axis=0)
    pre = tok[...].astype(f32) + dg(ctx.T, ow, 1, 0) + ob
    cen = pre - mean(pre)
    r1 = lax.rsqrt(mean(cen * cen) + 1e-6)
    n1 = cen * r1
    hid = n1 * g1 + s1
    hl = hid.astype(bf)
    hid_t[...] = hl.T
    acc = hid + db
    for j in range(J):
        u = dg(hl, U[j], 1, 0) + ub[j:j + 1, :]
        phi = 0.5 * lax.erf(u * 0.7071067811865476) + 0.5
        a = (u * phi).astype(bf)
        act[:, j * F:(j + 1) * F] = a
        G[:, j * F:(j + 1) * F] = phi + u * (jnp.exp2(u * u * -0.7213475204444817) * 0.3989422804014327)
        acc = acc + dg(a, Dn[j], 1, 0)
    cen = acc - mean(acc)
    r2 = lax.rsqrt(mean(cen * cen) + 1e-6)
    n2 = cen * r2
    out[...] = (n2 * g2 + s2).astype(bf)
    c = cot[...].astype(f32)
    csum(0, c * n2)
    csum(1, c)
    sg = c * g2
    gt = r2 * (sg - mean(sg) - n2 * mean(sg * n2))
    csum(2, gt)
    gl = gt.astype(bf)
    gl_t[...] = gl.T
    dh = gt
    for j in range(J):
        g = dg(gl, Dn[j], 1, 1) * G[:, j * F:(j + 1) * F]
        ubg[j:j + 1, :] += jnp.sum(g, axis=0, keepdims=True)
        gb = g.astype(bf)
        gu[:, j * F:(j + 1) * F] = gb
        dh = dh + dg(gb, U[j], 1, 1)
    csum(3, dh * n1)
    csum(4, dh)
    sg = dh * g1
    go = r1 * (sg - mean(sg) - n1 * mean(sg * n1))
    csum(5, go)
    g1_o[...] = go
    gol = go.astype(bf)
    gol_t[...] = gol.T
    do_t[...] = dg(ow, gol, 1, 1).astype(bf).reshape(do_t.shape)


def ffn(meta, u_own, d_own, pieces, layout, tok, cot, ctxs, wts, vec, ub, R=512):
    C, D = tok.shape
    J, F = ub.shape
    H = HEADS
    row = lambda w: pl.BlockSpec((R, w), lambda i: (i, 0))
    col = pl.BlockSpec((D, R), lambda i: (0, i))
    fix = lambda a: pl.BlockSpec(a.shape, lambda i: (0,) * a.ndim, pipeline_mode=pl.Buffered(1))
    hb = lambda n: pl.BlockSpec((n, HD, R), lambda i: (0, 0, i))
    acc = lambda s: pl.BlockSpec(s, lambda i: (0, 0))
    share = H // J * HD
    at = 3
    owb = lambda w: pl.BlockSpec((w.shape[0], share, D), lambda i: (0, at, 0), pipeline_mode=pl.Buffered(1))
    return pl.pallas_call(
        functools.partial(ffn_kernel, R=R, layout=layout), grid=(C // R,),
        in_specs=[SMEM, ANY, ANY] + [ANY] * len(pieces) + [row(D), row(D)] + [hb(c.shape[0]) for c in ctxs] + [owb(w) for w in wts] + [fix(vec), fix(ub)],
        out_specs=[row(D), row(J * F), row(J * F), col, col, row(D), col, hb(H), acc((8, D)), acc((J, F))],
        out_shape=[shape((C, D), bf), shape((C, J * F), bf), shape((C, J * F), bf), shape((D, C), bf), shape((D, C), bf), shape((C, D), f32),
                   shape((D, C), bf), shape((H, HD, C), bf), shape((8, D), f32), shape((J, F), f32)],
        scratch_shapes=[pltpu.VMEM((R, J * F), f32), pltpu.VMEM((J, D, F), bf), pltpu.VMEM((J, F, D), bf),
                        pltpu.SemaphoreType.DMA((2, J, len(pieces)))],
        compiler_params=params(60), cost_estimate=cost(2 * C * D * (2 * D + 4 * J * F), 60 * MIB), name="ffn",
    )(meta, u_own, d_own, *pieces, tok, cot, *ctxs, *wts, vec, ub)


def attn_bwd_kernel(meta, e, v_d, do_t, ctx, linv, q_t, k_t, cos, sin, gp, gb, D2, DI, DS, DST, ET, *, C, KC):
    length = meta[0, 0]
    g = do_t[...].astype(f32)
    inv = linv[...]
    DI[...] = jnp.sum(g * ctx[...].astype(f32), axis=0, keepdims=True) * inv
    g = g * inv
    hi = g.astype(bf)
    D2[:HD, :] = hi
    D2[HD:, :] = (g - hi.astype(f32)).astype(bf)
    for j in range(C // KC):
        r = slice(j * KC, (j + 1) * KC)
        dp = dg(v_d[r, :], D2[...], 1, 0)
        ej = e[r, :]
        ds = (ej.astype(f32) * (dp - DI[...])).astype(bf)
        DS[r, :] = ds
        DST[:, r] = ds.T
        ET[:, r] = ej.T
    dq = dg(k_t[...], DS[...], 1, 0)
    dk = dg(q_t[...], DST[...], 1, 0)
    dv = dg(D2[:HD, :], ET[...], 1, 0)
    live = lax.broadcasted_iota(jnp.int32, (HD, C), 1) < length
    c, s = cos[...], sin[...]

    def unrot(x):
        u, w = x[:HD // 2], x[HD // 2:]
        return jnp.concatenate([u * c + w * s, w * c - u * s], axis=0)

    def put(k, x):
        gp[k] = x.astype(bf)
        total = jnp.sum(x, axis=1, keepdims=True)
        gb[k:k + 1, :] = jnp.broadcast_to(total, (HD, 2 * HD)).T[:1]

    put(0, unrot(dq * 0.125))
    put(1, unrot(jnp.where(live, dk, 0.0)))
    put(2, jnp.where(live, dv, 0.0))


def attn_bwd(meta, saved, do_t, cos, sin, G, first, shift, H):
    e, v_d, ctx, linv, q_t, k_t = saved
    C = e.shape[1]
    sp = lambda s: pl.BlockSpec((None,) + s, lambda h: (h + first, 0, 0))
    tab = pl.BlockSpec((HD // 2, C), lambda h: (0, 0))
    return pl.pallas_call(
        functools.partial(attn_bwd_kernel, C=C, KC=min(256, C)), grid=(H,),
        in_specs=[SMEM, sp((C, C)), sp((C, 2 * HD)), pl.BlockSpec((None, HD, C), lambda h: (h + first + shift, 0, 0)), sp((HD, C)), sp((1, C)),
                  sp((HD, C)), sp((HD, C)), tab, tab],
        out_specs=[pl.BlockSpec((None, 3, None, HD, C), lambda h: (h // G, 0, h % G, 0, 0)), pl.BlockSpec((None, 3, HD), lambda h: (h, 0, 0))],
        out_shape=[shape((H // G, 3, G, HD, C), bf), shape((H, 3, HD), f32)],
        scratch_shapes=[pltpu.VMEM((2 * HD, C), bf), pltpu.VMEM((1, C), f32)] + [pltpu.VMEM((C, C), bf)] * 3,
        compiler_params=params(60), cost_estimate=cost(H * 8 * C * C * 256, H * C * C * 2 + 16 * MIB), name="attn_bwd",
    )(meta, e, v_d, do_t, ctx, linv, q_t, k_t, cos, sin)


NEAR = (0, 2, 4, 6)
SWAP = (0, 4, 2, 6)


def lay(meta, S, theirs, mine, rows, lanes, order):
    for i, rel in enumerate(order):
        for ref, low in ((mine, 0), (theirs, 1)):
            ref[i // 2, i % 2, 0, rows, lanes] = S[meta[0, 1] ^ (rel | low)].astype(bf)


def wgrad_d_kernel(meta, gl_t, act, vecs, theirs, mine, S):
    rows = S.shape[1]
    S[...] = dg(gl_t[...], act[...], 1, 0).reshape(S.shape)
    lay(meta, S, theirs, mine, slice(0, rows), slice(None), SWAP)
    for i, rel in enumerate(SWAP):
        for ref, low in ((mine, 0), (theirs, 1)):
            line = vecs[pl.ds(meta[0, 1] ^ (rel | low), 1), :]
            ref[i // 2, i % 2, 0, rows:, :] = jnp.broadcast_to(line, (EXTRA, line.shape[1])).astype(bf)


def wgrad_u_kernel(meta, hid_t, gu, gol_t, *refs):
    c0, c1, theirs, mine, S, SO = refs
    F = gu.shape[1]
    S[...] = dg(hid_t[...], gu[...], 1, 0).reshape(S.shape)
    lay(meta, S, theirs, mine, slice(None), slice(0, F), NEAR)

    def out(ctx):
        SO[...] = dg(gol_t[...], ctx[...].reshape(-1, ctx.shape[-1]), 1, 1).reshape(SO.shape)

    pl.when(pl.program_id(0) == 0)(lambda: out(c0))
    pl.when(pl.program_id(0) > 0)(lambda: out(c1))
    lay(meta, SO, theirs, mine, slice(None), slice(F, F + SO.shape[2]), NEAR)


def wgrad_q_kernel(meta, tok_t, gp, gb, theirs, mine, S):
    rows = S.shape[1]
    S[...] = dg(tok_t[...], gp[...], 1, 1).reshape(S.shape)
    lay(meta, S, theirs, mine, slice(0, rows), slice(None), SWAP)
    line = jnp.broadcast_to(gb[...], (EXTRA, gb.shape[1])).astype(bf)
    for i in range(4):
        for ref in (mine, theirs):
            ref[i // 2, i % 2, 0, rows:, :] = line


def wgrad(kernel, meta, args, specs, J, rows, lanes, scratch, name, flops):
    spec = pl.BlockSpec((2, 2, 1, rows, lanes), lambda j: (0, 0, j, 0, 0))
    return pl.pallas_call(
        kernel, grid=(J,), in_specs=[SMEM] + specs, out_specs=[spec] * 2, out_shape=[shape((2, 2, J, rows, lanes), bf)] * 2,
        scratch_shapes=[pltpu.VMEM(s, f32) for s in scratch],
        compiler_params=params(60), cost_estimate=cost(flops, 20 * MIB), name=name,
    )(meta, *args)


def final_du_kernel(meta, x, y, down, up, ow, small, S, SO):
    rows = S.shape[1]
    F = up.shape[1]
    for low, ref in enumerate((x, y)):
        for t, rel in enumerate(NEAR):
            at = meta[0, 1] ^ (rel | low)
            S[at] = ref[t, :rows, :F].astype(f32)
            small[pl.ds(at, 1), :] = ref[t, rows:rows + 1, :F].astype(f32)
            up[pl.ds(pl.multiple_of(at * rows, rows), rows), :] = ref[t, :rows, F:2 * F].astype(f32)
            SO[at] = ref[t, :rows, 2 * F:].astype(f32)
    down[...] = S[...].reshape(down.shape).T
    ow[...] = SO[...].reshape(-1, SO.shape[2]).T


def final_q_kernel(meta, x, y, qkv, gb):
    rows = x.shape[1] - EXTRA
    for low, ref in enumerate((x, y)):
        for t, rel in enumerate(NEAR):
            at = meta[0, 1] ^ (rel | low)
            qkv[pl.ds(pl.multiple_of(at * rows, rows), rows), :] = ref[t, :rows, :].astype(f32)
    gb[...] = x[0, rows:rows + 1, :].astype(f32)


def final(kernel, meta, xs, outs, scratch, name):
    return pl.pallas_call(
        kernel, in_specs=[SMEM] + [pl.BlockSpec(memory_space=pltpu.VMEM)] * 2,
        out_shape=[shape(s, f32) for s in outs], scratch_shapes=[pltpu.VMEM(s, f32) for s in scratch],
        compiler_params=params(60), cost_estimate=cost(0, 8 * MIB), name=name,
    )(meta, *xs)


def input_grad_kernel(*refs, N, n):
    gps, (w0, w1, g1, out) = refs[:n], refs[n:]
    acc = g1[...]
    j = 0
    for gp in gps:
        for i in range(gp.shape[0]):
            w = w0[0, :N, :] if j == 0 else w1[j - 1, :N, :]
            acc = acc + dg(gp[i], w, 0, 0)
            j += 1
    out[...] = acc


def input_grad(gps, w0, w1, g1, R=512):
    _, N, C = gps[0].shape
    D = g1.shape[1]
    fix = lambda a: pl.BlockSpec(a.shape, lambda i: (0,) * a.ndim, pipeline_mode=pl.Buffered(1))
    return pl.pallas_call(
        functools.partial(input_grad_kernel, N=N, n=len(gps)), grid=(C // R,),
        in_specs=[pl.BlockSpec((g.shape[0], N, R), lambda i: (0, 0, i)) for g in gps] + [fix(w0), fix(w1), pl.BlockSpec((R, D), lambda i: (i, 0))],
        out_specs=pl.BlockSpec((R, D), lambda i: (i, 0)), out_shape=shape((C, D), f32),
        compiler_params=params(60), cost_estimate=cost(2 * C * D * D * 3, 24 * MIB), name="input_grad",
    )(*gps, w0, w1, g1)


def fetch(x, s):
    n = lax.axis_size("narrow")
    return lax.ppermute(x, "narrow", [((i + s) % n, i) for i in range(n)])


def give(x, s):
    n = lax.axis_size("narrow")
    return lax.ppermute(x, "narrow", [(i, (i + s) % n) for i in range(n)])


def flip(x, bit):
    return lax.ppermute(x, "wide", [(i, i ^ bit) for i in range(lax.axis_size("wide"))])


def gather(x):
    x = jnp.stack([x] + [flip(x, rel) for rel in NEAR[1:]])
    return x, flip(x, 1)


def total(terms):
    x = terms[0].astype(f32)
    for y in terms[1:]:
        x = x + y.astype(f32)
    return x.astype(bf)


def rest(x):
    bit = SPLIT
    while bit < lax.axis_size("wide"):
        x = add(x, flip(x, bit))
        bit *= 2
    return x


def tie(xs, deps):
    return lax.optimization_barrier((xs, deps))[0]


def add(a, b):
    return (a.astype(f32) + b.astype(f32)).astype(bf)


def rotary_tables(capacity):
    positions = jnp.arange(capacity).astype(f32)
    frequencies = 10000.0 ** (-2.0 * jnp.arange(HD // 2).astype(f32) / HD)
    angles = frequencies[:, None] * positions[None, :]
    return jnp.cos(angles), jnp.sin(angles)


def shards(
    tokens, lengths, qkv_weight, qkv_bias, out_weight, out_bias, norm1_gain, norm1_shift,
    up_weight, up_bias, down_weight, down_bias, norm2_gain, norm2_shift, cotangent,
):
    J = lax.axis_size("narrow")
    tok, cot = tokens[0], cotangent[0]
    C, D = tok.shape
    G = HEADS // J
    N = 3 * G * HD
    F = up_weight.shape[1]
    rows = D // SPLIT
    low = jnp.bitwise_and(lax.axis_index("wide"), SPLIT - 1).astype(jnp.int32)
    length = lax.dynamic_slice(lengths, (0, lax.axis_index("narrow")), (1, 1))
    meta = jnp.concatenate([length, low.reshape(1, 1)], axis=1)
    cos, sin = rotary_tables(C)

    qo = jnp.concatenate([qkv_weight.reshape(D, N), out_weight.T], axis=1)
    bias = jnp.concatenate([qkv_bias.reshape(-1), up_bias])
    bias = jnp.pad(bias, (0, 2 * D - bias.size)).reshape(2, D)
    cut = lambda x: lax.dynamic_slice_in_dim(x, low * rows, rows, 0)
    q_piece = jnp.concatenate([cut(qo), jnp.pad(bias, ((0, EXTRA - 2), (0, 0)))], axis=0)
    got = [fetch(q_piece, s) for s in range(1, J)]
    vec = jnp.stack([out_bias, norm1_gain, norm1_shift, down_bias, norm2_gain, norm2_shift]).astype(f32)
    b_own = qkv_bias.astype(f32).reshape(1, 3, G, HD, 1)
    ud_piece = jnp.concatenate([cut(up_weight), cut(down_weight)], axis=1)
    ud_got = [fetch(tie(ud_piece, q_piece), 1)]
    q0, k0, v0, e0, c0, l0, wt0, tok_t = attn_fwd(meta, [qo[None]], ((None, 0, 0),), tok, b_own, cos, sin, True)
    got, ud_got, tok_t = lax.optimization_barrier((got, ud_got, tok_t))
    biases = jnp.stack([bias] + [x[rows:rows + 2] for x in got]).reshape(J, 2 * D).astype(f32)
    bq, ub = biases[1:, :N].reshape(J - 1, 3, G, HD, 1), biases[:, N:N + F]
    q = jnp.stack([x[:rows] for x in got])
    q_x, q_y = flip(q, 2), flip(q, 4)
    ud_2 = fetch(tie(ud_piece, got), 2)
    h = rows // 2
    q_x, q_y, ud_2 = lax.optimization_barrier((q_x, q_y, ud_2))
    q_d = [flip(q_y[:, :h], 2), flip(q_x[:, h:], 4)]
    q_far = [flip(x, 1) for x in (q, q_x, q_y)]
    ud_3 = fetch(tie(ud_piece, q_x), 3)
    q_d, ud_3 = lax.optimization_barrier((q_d, ud_3))
    q_far = q_far + [flip(x, 1) for x in q_d]
    q_pieces = [q, q_x, q_y] + q_d + q_far
    q_places = tuple((rel | low, half, rows) for low in (0, 1) for rel, half in ((0, 0), (2, 0), (4, 0), (6, 0), (6, h)))
    ud = jnp.stack(ud_got + [ud_2, ud_3])
    ud_near = [flip(ud, rel) for rel in NEAR[1:]]
    ud_far = [flip(ud, 1)]
    tok_t = tie(tok_t, ud)
    q1, k1, v1, e1, c1, l1, wt1 = attn_fwd(meta, q_pieces, q_places, tok_t, bq, cos, sin, False)
    ud_near, ud_far, c1 = lax.optimization_barrier((ud_near, ud_far, c1))
    ud_pieces = [ud] + ud_near + ud_far + [flip(x, 1) for x in ud_near]
    ud_places = [(rel | low, 0, rows) for low in (0, 1) for rel in NEAR]
    ud_layout = tuple(((0, 1), place) for place in ud_places)
    out, act, gu, hid_t, gl_t, g1, gol_t, do_t, small, ubg = ffn(
        meta, up_weight, down_weight, ud_pieces, ud_layout, tok, cot, (c0, c1), (wt0, wt1), vec, ub)

    whole = lambda a: pl.BlockSpec(a.shape, lambda j: (0,) * a.ndim, pipeline_mode=pl.Buffered(1))
    vecs = jnp.concatenate([jnp.broadcast_to(small[None, :6], (J, 6, D)), ubg[:, None], jnp.zeros((J, 1, D), f32)], axis=1)
    u_t, u_m = wgrad(
        wgrad_u_kernel, meta, (hid_t, gu, gol_t, c0, c1),
        [whole(hid_t), pl.BlockSpec((C, F), lambda j: (0, j)), whole(gol_t), pl.BlockSpec((G, HD, C), lambda j: (0, 0, 0)),
         pl.BlockSpec((G, HD, C), lambda j: (jnp.maximum(j - 1, 0), 0, 0))],
        J, rows, F + G * HD, [(SPLIT, rows, F), (SPLIT, rows, G * HD)], "wgrad_u", 2 * C * D * (J * F + D))
    u_1 = flip(u_t, 1)
    gl_t = tie(gl_t, u_t)
    d_t, d_m = wgrad(
        wgrad_d_kernel, meta, (gl_t, act, vecs),
        [whole(gl_t), pl.BlockSpec((C, F), lambda j: (0, j)), pl.BlockSpec((None, 8, D), lambda j: (j, 0, 0))],
        J, rows + EXTRA, F, [(SPLIT, rows, F)], "wgrad_d", 2 * C * D * J * F)

    def grad_q(gp, gb):
        n = gp.shape[0]
        return wgrad(
            wgrad_q_kernel, meta, (tok_t, gp, gb),
            [whole(tok_t), pl.BlockSpec((None, N, C), lambda j: (j, 0, 0)), pl.BlockSpec((None, 1, N), lambda j: (j, 0, 0))],
            n, rows + EXTRA, N, [(SPLIT, rows, N)], "wgrad_q", 2 * C * D * n * N)

    def backward(group, count, do_t):
        saved, shift = ((e0, v0, c0, l0, q0, k0), 0) if group == 0 else ((e1, v1, c1, l1, q1, k1), G)
        gp, gb = attn_bwd(meta, saved, do_t, cos, sin, G, group * G - shift, shift, count * G)
        return gp.reshape(count, N, C), gb.reshape(count, G, 3, HD).transpose(0, 2, 1, 3).reshape(count, 1, N)

    def halves(mine, got):
        return add(mine[0], got[0]), add(mine[1], got[1])

    u_1, u_m, d_t = lax.optimization_barrier((u_1, u_m, d_t))
    d_1 = flip(d_t, 1)
    u_k, u_s = halves(u_m, u_1)
    u_2 = flip(u_s, 4)
    do_t = tie(do_t, u_s)
    d_1, d_m, do_t = lax.optimization_barrier((d_1, d_m, do_t))
    d_k, d_s = halves(d_m, d_1)
    d_2 = flip(d_s, 2)
    do_t = tie(do_t, d_s)
    gpa, gba = backward(1, 2, do_t)
    u_2, d_2, gpa, do_t = lax.optimization_barrier((u_2, d_2, gpa, do_t))
    u_k, u_s = halves(u_k, u_2)
    u_3 = flip(u_s, 2)
    d_k, d_s = halves(d_k, d_2)
    d_3 = flip(d_s, 4)
    gpa_ = tie(gpa, (u_s, d_s))
    qa_t, qa_m = grad_q(gpa_, gba)
    qa_1 = flip(qa_t, 1)
    do_t = tie(do_t, qa_t)
    gpb, gbb = backward(0, 1, do_t)
    u_3, d_3, qa_1, gpb, do_t = lax.optimization_barrier((u_3, d_3, qa_1, gpb, do_t))
    du_s = [jnp.concatenate([add(d_k[j], d_3[j]), jnp.pad(add(u_k[j], u_3[j]), ((0, EXTRA), (0, 0)))], axis=1) for j in range(J)]
    du_3 = [give(du_s[s], s) for s in (1, 3)]
    qa_k, qa_s = halves(qa_m, qa_1)
    qa_2 = flip(qa_s, 2)
    do_t = tie(do_t, (du_s, qa_s))
    gpc, gbc = backward(3, 1, do_t)
    du_3, qa_2, gpb, gpc = lax.optimization_barrier((du_3, qa_2, gpb, gpc))
    du_3.append(give(tie(du_s[2], gpc), 2))
    qa_k, qa_s = halves(qa_k, qa_2)
    qa_3 = flip(qa_s, 4)
    gbc_ = jnp.stack([gpb[0], gpc[0]])
    gbc_ = tie(gbc_, (qa_s, qa_k))
    qb_t, qb_m = grad_q(gbc_, jnp.concatenate([gbb, gbc], axis=0))
    qb_1 = flip(qb_t, 1)
    qa_3, du_3, qb_m, qb_1 = lax.optimization_barrier((qa_3, du_3, qb_m, qb_1))
    qa_s = [add(qa_k[j], qa_3[j]) for j in range(2)]
    q_3 = [give(qa_s[0], 1), give(qa_s[1], 2)]
    du = rest(total([du_s[0]] + du_3))
    du_4 = [flip(du, rel) for rel in NEAR[1:]]
    qb_k, qb_s = halves(qb_m, qb_1)
    qb_2 = flip(qb_s, 2)
    g1 = tie(g1, (qb_k, qb_s, du, qa_s))
    x_grad = input_grad([gpb, gpa, gpc], wt0, wt1, g1)
    qb_2, qb_k, du_4, q_3 = tie((qb_2, qb_k, du_4, q_3), x_grad)
    qb_k, qb_s = halves(qb_k, qb_2)
    qb_3 = flip(qb_s, 4)
    du = jnp.stack([du] + du_4)
    du_5 = flip(du, 1)
    qb_3, du_5 = lax.optimization_barrier((qb_3, du_5))
    q_3 = [add(qb_k[0], qb_3[0])] + q_3 + [give(add(qb_k[1], qb_3[1]), J - 1)]
    q_sum = gather(rest(total(q_3)))
    down_g, up_g, ow_g, small = final(
        final_du_kernel, meta, (du, du_5), [(F, D), (D, F), (G * HD, D), (8, D)], [(SPLIT, rows, F), (SPLIT, rows, G * HD)], "final_du")
    qkv_g, gb = final(final_q_kernel, meta, q_sum, [(D, N), (1, N)], [], "final_q")
    return (
        out[None], x_grad[None], qkv_g.reshape(D, 3, G * HD), gb.reshape(3, G * HD), ow_g, small[5], small[3], small[4],
        up_g, small[6], down_g, small[2], small[0], small[1],
    )


def solution(mesh):
    rows = P(("wide", "narrow"), None, None)
    weights = (P(None, None, "narrow"), P(None, "narrow"), P("narrow", None), P(), P(), P(),
               P(None, "narrow"), P("narrow"), P("narrow", None), P(), P(), P())
    return jax.shard_map(
        shards, mesh=mesh, in_specs=(rows, P("wide", None)) + weights + (rows,),
        out_specs=(rows, rows) + weights, check_vma=False,
    )
```

time: 687 us -> 429 us (0.62)
  waiting for transfers between devices: 327 us -> 75.7 us
  Pallas kernels: 159 us -> 246 us
  blocking collectives: 81.6 us -> 0 us
  matrix products: 48.1 us -> 0 us
  starting transfers between devices: 1.04 us -> 41.9 us
  other arithmetic: 13.7 us -> 34.2 us
  between operations: 15.3 us -> 1.66 us
  local copies, waits for them, and re-layouts: 33.6 us -> 21.9 us
    all_gather x6 -> x0, waiting for transfers between devices: 172 us -> none  [the longest x4 159 us: gather_all(): full = lax.all_gather(piece, ('narrow', 'wide'), axis=0, tiled=True)]
    unnamed x16 -> x0, waiting for transfers between devices: 91.4 us -> none
    pallas_call x3 -> x13, Pallas kernels: 159 us -> 246 us  [the longest x2 69.2 us: attn_fwd(): pl.pallas_call(functools.partial(attn_fwd_kernel, C=C, KC=min(128, C), G=...]
    ppermute x0 -> x48, waiting for transfers between devices: none -> 75.7 us  [the longest x36 41.1 us: flip(): lax.ppermute(x, 'wide', [(i, i ^ bit) for i in range(lax.axis_size('wide'...]
    reduce_scatter x6 -> x0, waiting for transfers between devices: 63.9 us -> none  [the longest x4 44.7 us: reduce_all(): part = lax.psum_scatter(part, 'narrow', scatter_dimension=0, tiled=True)]
    dot_general x8 -> x0, matrix products: 48.1 us -> none  [dg(): lax.dot_general(a, b, (((ca,), (cb,)), ((), ())), preferred_element_type=...]
    ppermute x0 -> x48, starting transfers between devices: none -> 41.9 us  [the longest x36 23.8 us: flip(): lax.ppermute(x, 'wide', [(i, i ^ bit) for i in range(lax.axis_size('wide'...]
    psum x1 -> x0, blocking collectives: 39.6 us -> none  [shards(): packed = lax.psum(packed, ('wide', 'narrow'))]
  transfers between devices with their start and end apart: 14 -> 48, of which waited for: 10 -> 19; matrix products, arithmetic and copies ran while one was open for 11% -> 8% of each run, Pallas kernels for 16% -> 38%
where the time goes in v2:
time: 429 us; the launch traced here: 422 us
  Pallas kernels  246 us (57%)
  waiting for transfers between devices  75.7 us (18%)
  starting transfers between devices  41.9 us (10%)
  other arithmetic  34.2 us (8%)
  local copies, waits for them, and re-layouts  21.9 us (5%)
    pallas_call x2, Pallas kernels, attn_fwd(): pl.pallas_call(functools.partial(attn_fwd_kernel, C=C, KC=min(128, C), G=...  69.2 us
    pallas_call x3, Pallas kernels, attn_bwd(): pl.pallas_call(functools.partial(attn_bwd_kernel, C=C, KC=min(256, C)), g...  61.3 us
    pallas_call x1, Pallas kernels, ffn(): pl.pallas_call(functools.partial(ffn_kernel, R=R, layout=layout), grid=(C...  51.1 us
    pallas_call x4, Pallas kernels, wgrad(): pl.pallas_call(kernel, grid=(J,), in_specs=[SMEM] + specs, out_specs=[spe...  43.8 us
    ppermute x36, waiting for transfers between devices, flip(): lax.ppermute(x, 'wide', [(i, i ^ bit) for i in range(lax.axis_size('wide'...  41.1 us
    ppermute x36, starting transfers between devices, flip(): lax.ppermute(x, 'wide', [(i, i ^ bit) for i in range(lax.axis_size('wide'...  23.8 us
    convert_element_type x12, other arithmetic, add(): return (a.astype(f32) + b.astype(f32)).astype(bf)  20 us
    ppermute x6, waiting for transfers between devices, give(): return lax.ppermute(x, 'narrow', [(i, (i + s) % n) for i in range(n)])  19.7 us
  transfers between devices with their start and end apart: 48, of which 19 were waited for; matrix products, arithmetic and copies ran while one was open for 8% of the time, Pallas kernels for 38%

profile of v2, /device:TPU:0, one launch (start us, length us, event | category | flops | bytes accessed | tf_op | source)
XLA Modules:
  0.0 421.6 jit_solution(1323254588376443737)
XLA Ops:
  0.7 1.6 copy.37
  2.8 5.1 %collective-permute-start = (bf16[104,768]{1,0:T(8,128)(2,1)S(1)}, bf16[104,768]{1,0:T(8,128)(2,1)S(1)}, u32[]{:S(2)}, u32[]{:S(2)}) collective-permute-start(bf16[104,768]{1,0:T(8,128)(2,1)S(1)} %fusion.44), channel_id=1, source_target_pairs={{1,0},{2,1},{3,2},{0,3},{5,4},{6,5},{7,6},{4,7},{9,8},{10,9},{11,1... | collective-permute-start | bytes 479240 | tf_op jit(solution)/shard_map/ppermute | solution.py:429
  7.9 1.0 collective-permute-start.2
  8.9 1.0 constant_dynamic-slice_fusion
  10.6 2.8 collective-permute-start.3
  13.5 1.5 multiply_sine_fusion
  15.6 1.2 pad_add_fusion.meta
  16.8 0.9 reshape.308.refs_2_
  17.7 1.2 fusion.6.refs_0_
  19.0 21.0 %attn_fwd_own.1 = (bf16[3,64,1536]{2,1,0:T(8,128)(2,1)}, bf16[3,64,1536]{2,1,0:T(8,128)(2,1)}, bf16[3,1536,128]{2,1,0:T(8,128)(2,1)}, bf16[3,1536,1536]{2,1,0:T(...) custom-call(s32[1,2]{1,0:T(1,128)} %pad_add_fusion.meta, ...), custom_call_target="tpu_custom_call" | custom-call | flops 1 | bytes 1 | tf_op jit(solution)/shard_map/attn_fwd_own/pallas_call | solution.py:149
  40.8 1.5 collective-permute-start.4
  42.3 1.5 collective-permute-start.5
  43.9 1.1 collective-permute-start.6
  45.0 11.6 %collective-permute-done.6 = bf16[96,1536]{1,0:T(8,128)(2,1)S(1)} collective-permute-done((bf16[96,1536]{1,0:T(8,128)(2,1)}, bf16[96,1536]{1,0:T(8,128)(2,1)S(1)}, u32[]{:S(2)}, u32[]{:S(2)}) %collective-permute-start.6) | collective-permute-done | bytes 294944 | tf_op jit(solution)/shard_map/ppermute | solution.py:429
  58.5 6.0 %collective-permute-done.7.refs_3_ = bf16[3,48,768]{2,1,0:T(8,128)(2,1)S(1)} collective-permute-done((bf16[3,48,768]{2,1,0:T(8,128)(2,1)S(1)}, bf16[3,48,768]{2,1,0:T(8,128)(2,1)S(1)}, u32[]{:S(2)}, u32[]{:S(2)}) %collective-permute-start.7) | collective-permute-done | bytes 221216 | tf_op jit(solution)/shard_map/ppermute | solution.py:438
  64.9 3.2 collective-permute-done.9
  68.6 3.1 collective-permute-start.12
  77.3 2.4 reshape.309.refs_11_
  79.8 48.2 %attn_fwd.1 = (bf16[9,64,1536]{2,1,0:T(8,128)(2,1)}, bf16[9,64,1536]{2,1,0:T(8,128)(2,1)}, bf16[9,1536,128]{2,1,0:T(8,128)(2,1)}, bf16[9,1536,1536]{2,1,0:T(8,12...) custom-call(s32[1,2]{1,0:T(1,128)} %pad_add_fusion.meta, ...), custom_call_target="tpu_custom_call" | custom-call | flops 1 | bytes 1 | tf_op jit(solution)/shard_map/attn_fwd/pallas_call | solution.py:149
  130.1 0.8 collective-permute-done.19.refs_5_
  131.0 1.9 collective-permute-done.20.refs_6_
  133.8 51.1 %ffn.1 = (bf16[1536,768]{1,0:T(8,128)(2,1)}, bf16[1536,3072]{1,0:T(8,128)(2,1)}, bf16[1536,3072]{1,0:T(8,128)(2,1)}, bf16[768,1536]{1,0:T(8,128)(2,1)}, bf16[768...) custom-call(s32[1,2]{1,0:T(1,128)} %pad_add_fusion.meta, ...), custom_call_target="tpu_custom_call" | custom-call | flops 1 | bytes 1 | tf_op jit(solution)/shard_map/ffn/pallas_call | solution.py:254
  184.9 16.6 %wgrad_u.1 = (bf16[2,2,4,96,960]{4,3,2,1,0:T(8,128)(2,1)}, bf16[2,2,4,96,960]{4,3,2,1,0:T(8,128)(2,1)}) custom-call(s32[1,2]{1,0:T(1,128)} %pad_add_fusion.meta, bf16[768,1536]{1,0:T(8,128)(2,1)} %get-tuple-element.149.hid_t, bf16[1536,3072]{1,0:T(8,128)(2,1)} %get-tuple-element.150.gu, bf16[768,1536]{1,0:T(8,128)(2,1)} %get-tuple-element.151.gol_t, ...), custom_call_target="tpu_custom_call" | custom-call | flops 1 | bytes 1 | tf_op jit(solution)/shard_map/wgrad_u/pallas_call | solution.py:365
  202.7 12.2 %wgrad_d.1 = (bf16[2,2,4,104,768]{4,3,2,1,0:T(8,128)(2,1)}, bf16[2,2,4,104,768]{4,3,2,1,0:T(8,128)(2,1)}) custom-call(s32[1,2]{1,0:T(1,128)} %pad_add_fusion.meta, bf16[768,1536]{1,0:T(8,128)(2,1)} %get-tuple-element.155.gl_t, bf16[1536,3072]{1,0:T(8,128)(2,1)} %get-tuple-element.156.act, f32[4,8,768]{2,1,0:T(8,128)} %maximum_maximum_fusion.vecs), custom_call_target="tpu_custom_call" | custom-call | flops 1 | bytes 1 | tf_op jit(solution)/shard_map/wgrad_d/pallas_call | solution.py:365
  214.9 1.7 copy-done.5
  216.7 5.8 %fusion = (bf16[2,4,96,960]{3,2,1,0:T(8,128)(2,1)}, bf16[1,2,4,96,960]{4,3,2,1,0:T(8,128)(2,1)S(1)}) fusion(bf16[2,2,4,96,960]{4,3,2,1,0:T(8,128)(2,1)} %copy-done.5, bf16[2,2,4,96,960]{4,3,2,1,0:T(8,128)(2,1)} %get-tuple-element.163), kind=kLoop, calls=%fused_computation.5 | loop fusion | flops 5898240 | bytes 8847360 | tf_op jit(solution)/shard_map/convert_element_type | solution.py:466
  222.5 1.7 add_convert_fusion.3
  224.2 2.6 collective-permute-start.25
  226.8 28.5 %attn_bwd.3 = (bf16[2,3,3,64,1536]{4,3,2,1,0:T(8,128)(2,1)}, f32[6,3,64]{2,1,0:T(4,128)}) custom-call(s32[1,2]{1,0:T(1,128)} %pad_add_fusion.meta, bf16[9,1536,1536]{2,1,0:T(8,128)(2,1)} %get-tuple-element.168.e, bf16[9,1536,128]{2,1,0:T(8,128)(2,1)} %get-tuple-element.169.v_d, bf16[12,64,1536]{2,1,0:T(8,128)(2,1)} %get-tuple-element.196.do_t, ...), custom_call_target="tpu_custom_call" | custom-call | flops 1 | bytes 1 | tf_op jit(solution)/shard_map/attn_bwd/pallas_call | solution.py:308
  256.7 2.8 collective-permute-done.24
  259.5 2.4 fusion.5
  261.9 3.0 fusion.7
  265.0 7.5 %wgrad_q.2 = (bf16[2,2,2,104,576]{4,3,2,1,0:T(8,128)(2,1)}, bf16[2,2,2,104,576]{4,3,2,1,0:T(8,128)(2,1)}) custom-call(s32[1,2]{1,0:T(1,128)} %pad_add_fusion.meta, bf16[768,1536]{1,0:T(8,128)(2,1)} %get-tuple-element.138.refs_10_.tok_t, bf16[2,576,1536]{2,1,0:T(8,128)(2,1)} %bitcast.189, f32[2,1,576]{2,1,0:T(1,128)} %reshape.310.gb), custom_call_target="tpu_custom_call" | custom-call | flops 1 | bytes 1 | tf_op jit(solution)/shard_map/wgrad_q/pallas_call | solution.py:365
  273.1 1.8 collective-permute-start.27
  274.9 16.5 %attn_bwd.4 = (bf16[1,3,3,64,1536]{4,3,2,1,0:T(8,128)(2,1)}, f32[3,3,64]{2,1,0:T(4,128)}) custom-call(s32[1,2]{1,0:T(1,128)} %pad_add_fusion.meta, bf16[3,1536,1536]{2,1,0:T(8,128)(2,1)} %get-tuple-element.182.e, bf16[3,1536,128]{2,1,0:T(8,128)(2,1)} %get-tuple-element.183.v_d, bf16[12,64,1536]{2,1,0:T(8,128)(2,1)} %get-tuple-element.196.do_t, ...), custom_call_target="tpu_custom_call" | custom-call | flops 1 | bytes 1 | tf_op jit(solution)/shard_map/attn_bwd/pallas_call | solution.py:308
  291.4 1.3 collective-permute-done.26
  292.8 1.3 add_convert_fusion.6
  294.7 1.3 fusion.47
  296.0 1.5 fusion.42
  298.3 3.6 collective-permute-start.30
  302.9 16.3 %attn_bwd.5 = (bf16[1,3,3,64,1536]{4,3,2,1,0:T(8,128)(2,1)}, f32[3,3,64]{2,1,0:T(4,128)}) custom-call(s32[1,2]{1,0:T(1,128)} %pad_add_fusion.meta, bf16[9,1536,1536]{2,1,0:T(8,128)(2,1)} %get-tuple-element.168.e, bf16[9,1536,128]{2,1,0:T(8,128)(2,1)} %get-tuple-element.169.v_d, bf16[12,64,1536]{2,1,0:T(8,128)(2,1)} %get-tuple-element.196.do_t, ...), custom_call_target="tpu_custom_call" | custom-call | flops 1 | bytes 1 | tf_op jit(solution)/shard_map/attn_bwd/pallas_call | solution.py:308
  320.6 3.7 pad_maximum_fusion.gp
  324.2 1.2 fusion.16
  325.4 7.5 %wgrad_q.3 = (bf16[2,2,2,104,576]{4,3,2,1,0:T(8,128)(2,1)}, bf16[2,2,2,104,576]{4,3,2,1,0:T(8,128)(2,1)}) custom-call(s32[1,2]{1,0:T(1,128)} %pad_add_fusion.meta, bf16[768,1536]{1,0:T(8,128)(2,1)} %get-tuple-element.138.refs_10_.tok_t, bf16[2,576,1536]{2,1,0:T(8,128)(2,1)} %pad_maximum_fusion.gp, f32[2,1,576]{2,1,0:T(1,128)} %pad_maximum_fusion.10.gb), custom_call_target="tpu_custom_call" | custom-call | flops 1 | bytes 1 | tf_op jit(solution)/shard_map/wgrad_q/pallas_call | solution.py:365
  332.9 1.9 collective-permute-start.33
  335.3 8.0 %collective-permute-done.32 = bf16[2,104,576]{2,1,0:T(8,128)(2,1)S(1)} collective-permute-done((bf16[2,104,576]{2,1,0:T(8,128)(2,1)S(1)}, bf16[2,104,576]{2,1,0:T(8,128)(2,1)S(1)}, u32[]{:S(2)}, u32[]{:S(2)}) %collective-permute-start.32) | collective-permute-done | bytes 239648 | tf_op jit(solution)/shard_map/ppermute | solution.py:438
  343.2 9.6 %collective-permute-done.33 = bf16[104,1728]{1,0:T(8,128)(2,1)S(1)} collective-permute-done((bf16[104,1728]{1,0:T(8,128)(2,1)S(1)}, bf16[104,1728]{1,0:T(8,128)(2,1)S(1)}, u32[]{:S(2)}, u32[]{:S(2)}) %collective-permute-start.33) | collective-permute-done | bytes 359456 | tf_op jit(solution)/shard_map/ppermute | solution.py:434
  352.9 1.5 fusion.15
  354.9 1.8 collective-permute-start.36
  356.7 1.7 collective-permute-start.37
  358.6 6.8 %collective-permute-done.39 = bf16[104,576]{1,0:T(8,128)(2,1)S(1)} collective-permute-done((bf16[104,576]{1,0:T(8,128)(2,1)S(1)}, bf16[104,576]{1,0:T(8,128)(2,1)S(1)}, u32[]{:S(2)}, u32[]{:S(2)}) %collective-permute-start.39) | collective-permute-done | bytes 119840 | tf_op jit(solution)/shard_map/ppermute | solution.py:434
  365.4 13.3 %input_grad.1 = f32[1536,768]{1,0:T(8,128)} custom-call(bf16[1,576,1536]{2,1,0:T(8,128)(2,1)} %bitcast.193, bf16[2,576,1536]{2,1,0:T(8,128)(2,1)} %bitcast.190, bf16[1,576,1536]{2,1,0:T(8,128)(2,1)} %bitcast.196, bf16[1,768,768]{2,1,0:T(8,128)(2,1)} %get-tuple-element.146.refs_12_.refs_3_, bf16[3,768,768]{2,1,0:T(8,128)(2,1)} %get-tuple-element.147.refs_13_.refs_4_, ...), custom_call_target="tpu_custom_call" | custom-call | flops 1 | bytes 1 | tf_op jit(solution)/shard_map/input_grad/pallas_call | solution.py:419
  378.7 6.6 %collective-permute-done.38 = bf16[104,1728]{1,0:T(8,128)(2,1)S(1)} collective-permute-done((bf16[104,1728]{1,0:T(8,128)(2,1)S(1)}, bf16[104,1728]{1,0:T(8,128)(2,1)S(1)}, u32[]{:S(2)}, u32[]{:S(2)}) %collective-permute-start.38) | collective-permute-done | bytes 359456 | tf_op jit(solution)/shard_map/ppermute | solution.py:438
  386.0 8.5 %collective-permute-done.41 = bf16[2,104,576]{2,1,0:T(8,128)(2,1)S(1)} collective-permute-done((bf16[2,104,576]{2,1,0:T(8,128)(2,1)S(1)}, bf16[2,104,576]{2,1,0:T(8,128)(2,1)S(1)}, u32[]{:S(2)}, u32[]{:S(2)}) %collective-permute-start.41) | collective-permute-done | bytes 239648 | tf_op jit(solution)/shard_map/ppermute | solution.py:438
  394.6 1.9 collective-permute-start.43
  396.5 3.3 collective-permute-done.43
  400.3 0.9 collective-permute-start.45
  401.2 2.3 collective-permute-start.46
  403.5 2.2 collective-permute-done.44
  405.9 1.4 collective-permute-done.46
  407.6 5.2 %final_du.1 = (f32[768,768]{1,0:T(8,128)}, f32[768,768]{1,0:T(8,128)}, f32[192,768]{1,0:T(8,128)}, f32[8,768]{1,0:T(8,128)}) custom-call(s32[1,2]{1,0:T(1,128)} %pad_add_fusion.meta, bf16[4,104,1728]{2,1,0:T(8,128)(2,1)} %copy-done.3, bf16[4,104,1728]{2,1,0:T(8,128)(2,1)} %copy-done.10), custom_call_target="tpu_custom_call" | custom-call | flops 1 | bytes 1 | tf_op jit(solution)/shard_map/final_du/pallas_call | solution.py:396
  412.7 1.8 slice_reduce_fusion
  415.3 2.6 final_q.1
  418.0 2.8 copy.44
  (211 shorter events, 25.2 us)
Async XLA Ops:
  2.8 37.2 %collective-permute-start = (bf16[104,768]{1,0:T(8,128)(2,1)S(1)}, bf16[104,768]{1,0:T(8,128)(2,1)S(1)}, u32[]{:S(2)}, u32[]{:S(2)}) collective-permute-start(bf16[104,768]{1,0:T(8,128)(2,1)S(1)} %fusion.44), channel_id=1, source_target_pairs={{1,0},{2,1},{3,2},{0,3},{5,4},{6,5},{7,6},{4,7},{9,8},{10,9},{11,1... | collective-permute-start | bytes 479240 | tf_op jit(solution)/shard_map/ppermute | solution.py:429
  7.9 32.1 %collective-permute-start.1 = (bf16[104,768]{1,0:T(8,128)(2,1)S(1)}, bf16[104,768]{1,0:T(8,128)(2,1)S(1)}, u32[]{:S(2)}, u32[]{:S(2)}) collective-permute-start(bf16[104,768]{1,0:T(8,128)(2,1)S(1)} %fusion.44), channel_id=1, source_target_pairs={{2,0},{3,1},{0,2},{1,3},{6,4},{7,5},{4,6},{5,7},{10,8},{11,9},{8,1... | collective-permute-start | bytes 479240 | tf_op jit(solution)/shard_map/ppermute | solution.py:429
  7.9 32.1 %collective-permute-start.2 = (bf16[104,768]{1,0:T(8,128)(2,1)S(1)}, bf16[104,768]{1,0:T(8,128)(2,1)S(1)}, u32[]{:S(2)}, u32[]{:S(2)}) collective-permute-start(bf16[104,768]{1,0:T(8,128)(2,1)S(1)} %fusion.44), channel_id=1, source_target_pairs={{3,0},{0,1},{1,2},{2,3},{7,4},{4,5},{5,6},{6,7},{11,8},{8,9},{9,10... | collective-permute-start | bytes 479240 | tf_op jit(solution)/shard_map/ppermute | solution.py:429
  10.6 29.4 %collective-permute-start.3 = (bf16[96,1536]{1,0:T(8,128)(2,1)}, bf16[96,1536]{1,0:T(8,128)(2,1)S(1)}, u32[]{:S(2)}, u32[]{:S(2)}) collective-permute-start(bf16[96,1536]{1,0:T(8,128)(2,1)} %pad_maximum_fusion.6), channel_id=1, source_target_pairs={{1,0},{2,1},{3,2},{0,3},{5,4},{6,5},{7,6},{4,7},{9,8},{10,9},{11,1... | collective-permute-start | bytes 884744 | tf_op jit(solution)/shard_map/ppermute | solution.py:429
  40.8 38.9 %copy-start.9 = (bf16[3,96,768]{2,1,0:T(8,128)(2,1)}, bf16[3,96,768]{2,1,0:T(8,128)(2,1)S(1)}, u32[]{:S(2)}) copy-start(bf16[3,96,768]{2,1,0:T(8,128)(2,1)S(1)} %pad_maximum_fusion.5.refs_0_) | copy-start | bytes 1327108
  40.8 15.8 %collective-permute-start.4 = (bf16[3,96,768]{2,1,0:T(8,128)(2,1)S(1)}, bf16[3,96,768]{2,1,0:T(8,128)(2,1)S(1)}, u32[]{:S(2)}, u32[]{:S(2)}) collective-permute-start(bf16[3,96,768]{2,1,0:T(8,128)(2,1)S(1)} %pad_maximum_fusion.5.refs_0_), channel_id=1, source_target_pairs={{0,8},{4,12},{8,0},{12,4},{16,24},{20,28},{24,16},{28,20},{1,9},{5... | collective-permute-start | bytes 1327112 | tf_op jit(solution)/shard_map/ppermute | solution.py:438
  42.3 14.2 %collective-permute-start.5 = (bf16[3,96,768]{2,1,0:T(8,128)(2,1)S(1)}, bf16[3,96,768]{2,1,0:T(8,128)(2,1)S(1)}, u32[]{:S(2)}, u32[]{:S(2)}) collective-permute-start(bf16[3,96,768]{2,1,0:T(8,128)(2,1)S(1)} %pad_maximum_fusion.5.refs_0_), channel_id=1, source_target_pairs={{0,16},{4,20},{8,24},{12,28},{16,0},{20,4},{24,8},{28,12},{1,17},{... | collective-permute-start | bytes 1327112 | tf_op jit(solution)/shard_map/ppermute | solution.py:438
  43.9 12.7 %collective-permute-start.6 = (bf16[96,1536]{1,0:T(8,128)(2,1)}, bf16[96,1536]{1,0:T(8,128)(2,1)S(1)}, u32[]{:S(2)}, u32[]{:S(2)}) collective-permute-start(bf16[96,1536]{1,0:T(8,128)(2,1)} %pad_maximum_fusion.6), channel_id=1, source_target_pairs={{2,0},{3,1},{0,2},{1,3},{6,4},{7,5},{4,6},{5,7},{10,8},{11,9},{8,1... | collective-permute-start | bytes 884744 | tf_op jit(solution)/shard_map/ppermute | solution.py:429
  56.5 23.1 %copy-start.12 = (bf16[3,96,768]{2,1,0:T(8,128)(2,1)}, bf16[3,96,768]{2,1,0:T(8,128)(2,1)S(1)}, u32[]{:S(2)}) copy-start(bf16[3,96,768]{2,1,0:T(8,128)(2,1)S(1)} %collective-permute-done.4.refs_1_) | copy-start | bytes 1327108
  56.5 23.1 %copy-start.13 = (bf16[3,96,768]{2,1,0:T(8,128)(2,1)}, bf16[3,96,768]{2,1,0:T(8,128)(2,1)S(1)}, u32[]{:S(2)}) copy-start(bf16[3,96,768]{2,1,0:T(8,128)(2,1)S(1)} %collective-permute-done.5.refs_2_) | copy-start | bytes 1327108
  56.6 11.5 %collective-permute-start.9 = (bf16[96,1536]{1,0:T(8,128)(2,1)}, bf16[96,1536]{1,0:T(8,128)(2,1)S(1)}, u32[]{:S(2)}, u32[]{:S(2)}) collective-permute-start(bf16[96,1536]{1,0:T(8,128)(2,1)} %pad_maximum_fusion.6), channel_id=1, source_target_pairs={{3,0},{0,1},{1,2},{2,3},{7,4},{4,5},{5,6},{6,7},{11,8},{8,9},{9,10... | collective-permute-start | bytes 884744 | tf_op jit(solution)/shard_map/ppermute | solution.py:429
  57.2 7.4 %collective-permute-start.7 = (bf16[3,48,768]{2,1,0:T(8,128)(2,1)S(1)}, bf16[3,48,768]{2,1,0:T(8,128)(2,1)S(1)}, u32[]{:S(2)}, u32[]{:S(2)}) collective-permute-start(bf16[3,48,768]{2,1,0:T(8,128)(2,1)S(1)} %slice.243), channel_id=1, source_target_pairs={{0,8},{4,12},{8,0},{12,4},{16,24},{20,28},{24,16},{28,20},{1,9},{5... | collective-permute-start | bytes 663560 | tf_op jit(solution)/shard_map/ppermute | solution.py:438
  57.6 7.2 %collective-permute-start.8 = (bf16[3,48,768]{2,1,0:T(8,128)(2,1)S(1)}, bf16[3,48,768]{2,1,0:T(8,128)(2,1)}, u32[]{:S(2)}, u32[]{:S(2)}) collective-permute-start(bf16[3,48,768]{2,1,0:T(8,128)(2,1)S(1)} %slice.244), channel_id=1, source_target_pairs={{0,16},{4,20},{8,24},{12,28},{16,0},{20,4},{24,8},{28,12},{1,17},{... | collective-permute-start | bytes 663560 | tf_op jit(solution)/shard_map/ppermute | solution.py:438
  58.0 10.6 %collective-permute-start.14 = (bf16[3,96,768]{2,1,0:T(8,128)(2,1)S(1)}, bf16[3,96,768]{2,1,0:T(8,128)(2,1)S(1)}, u32[]{:S(2)}, u32[]{:S(2)}) collective-permute-start(bf16[3,96,768]{2,1,0:T(8,128)(2,1)S(1)} %pad_maximum_fusion.5.refs_0_), channel_id=1, source_target_pairs={{0,4},{4,0},{8,12},{12,8},{16,20},{20,16},{24,28},{28,24},{1,5},{5... | collective-permute-start | bytes 1327112 | tf_op jit(solution)/shard_map/ppermute | solution.py:438
  58.0 13.7 %collective-permute-start.15 = (bf16[3,96,768]{2,1,0:T(8,128)(2,1)S(1)}, bf16[3,96,768]{2,1,0:T(8,128)(2,1)S(1)}, u32[]{:S(2)}, u32[]{:S(2)}) collective-permute-start(bf16[3,96,768]{2,1,0:T(8,128)(2,1)S(1)} %collective-permute-done.4.refs_1_), channel_id=1, source_target_pairs={{0,4},{4,0},{8,12},{12,8},{16,20},{20,16},{24,28},{28,24},{1,5},{5... | collective-permute-start | bytes 1327112 | tf_op jit(solution)/shard_map/ppermute | solution.py:438
  64.6 7.9 %collective-permute-start.16 = (bf16[3,96,768]{2,1,0:T(8,128)(2,1)S(1)}, bf16[3,96,768]{2,1,0:T(8,128)(2,1)S(1)}, u32[]{:S(2)}, u32[]{:S(2)}) collective-permute-start(bf16[3,96,768]{2,1,0:T(8,128)(2,1)S(1)} %collective-permute-done.5.refs_2_), channel_id=1, source_target_pairs={{0,4},{4,0},{8,12},{12,8},{16,20},{20,16},{24,28},{28,24},{1,5},{5... | collective-permute-start | bytes 1327112 | tf_op jit(solution)/shard_map/ppermute | solution.py:438
  68.2 59.8 %copy-start.4 = (bf16[3,96,1536]{2,1,0:T(8,128)(2,1)}, bf16[3,96,1536]{2,1,0:T(8,128)(2,1)S(1)}, u32[]{:S(2)}) copy-start(bf16[3,96,1536]{2,1,0:T(8,128)(2,1)S(1)} %pad_maximum_fusion.3.refs_0_) | copy-start | bytes 2654212
  68.2 59.8 %collective-permute-start.10 = (bf16[3,96,1536]{2,1,0:T(8,128)(2,1)S(1)}, bf16[3,96,1536]{2,1,0:T(8,128)(2,1)S(1)}, u32[]{:S(2)}, u32[]{:S(2)}) collective-permute-start(bf16[3,96,1536]{2,1,0:T(8,128)(2,1)S(1)} %pad_maximum_fusion.3.refs_0_), channel_id=1, source_target_pairs={{0,8},{4,12},{8,0},{12,4},{16,24},{20,28},{24,16},{28,20},{1,9},{5... | collective-permute-start | bytes 2654216 | tf_op jit(solution)/shard_map/ppermute | solution.py:438
  68.6 59.4 %collective-permute-start.11 = (bf16[3,96,1536]{2,1,0:T(8,128)(2,1)S(1)}, bf16[3,96,1536]{2,1,0:T(8,128)(2,1)}, u32[]{:S(2)}, u32[]{:S(2)}) collective-permute-start(bf16[3,96,1536]{2,1,0:T(8,128)(2,1)S(1)} %pad_maximum_fusion.3.refs_0_), channel_id=1, source_target_pairs={{0,16},{4,20},{8,24},{12,28},{16,0},{20,4},{24,8},{28,12},{1,17},{... | collective-permute-start | bytes 2654216 | tf_op jit(solution)/shard_map/ppermute | solution.py:438
  68.6 59.4 %collective-permute-start.12 = (bf16[3,96,1536]{2,1,0:T(8,128)(2,1)S(1)}, bf16[3,96,1536]{2,1,0:T(8,128)(2,1)}, u32[]{:S(2)}, u32[]{:S(2)}) collective-permute-start(bf16[3,96,1536]{2,1,0:T(8,128)(2,1)S(1)} %pad_maximum_fusion.3.refs_0_), channel_id=1, source_target_pairs={{0,24},{4,28},{8,16},{12,20},{16,8},{20,12},{24,0},{28,4},{1,25},{... | collective-permute-start | bytes 2654216 | tf_op jit(solution)/shard_map/ppermute | solution.py:438
  71.7 56.3 %collective-permute-start.13 = (bf16[3,96,1536]{2,1,0:T(8,128)(2,1)S(1)}, bf16[3,96,1536]{2,1,0:T(8,128)(2,1)}, u32[]{:S(2)}, u32[]{:S(2)}) collective-permute-start(bf16[3,96,1536]{2,1,0:T(8,128)(2,1)S(1)} %pad_maximum_fusion.3.refs_0_), channel_id=1, source_target_pairs={{0,4},{4,0},{8,12},{12,8},{16,20},{20,16},{24,28},{28,24},{1,5},{5... | collective-permute-start | bytes 2654216 | tf_op jit(solution)/shard_map/ppermute | solution.py:438
  72.5 1.9 collective-permute-start.17
  75.2 4.6 %collective-permute-start.18 = (bf16[3,48,768]{2,1,0:T(8,128)(2,1)}, bf16[3,48,768]{2,1,0:T(8,128)(2,1)}, u32[]{:S(2)}, u32[]{:S(2)}) collective-permute-start(bf16[3,48,768]{2,1,0:T(8,128)(2,1)} %collective-permute-done.8.refs_4_), channel_id=1, source_target_pairs={{0,4},{4,0},{8,12},{12,8},{16,20},{20,16},{24,28},{28,24},{1,5},{5... | collective-permute-start | bytes 663560 | tf_op jit(solution)/shard_map/ppermute | solution.py:438
  79.7 49.0 %copy-start.38 = (bf16[768]{0:T(1024)(128)(2,1)S(1)}, bf16[768]{0:T(1024)(128)(2,1)}, u32[]{:S(2)}) copy-start(bf16[768]{0:T(1024)(128)(2,1)} %param.20) | copy-start | bytes 4612
  79.7 49.0 %copy-start.39 = (bf16[768]{0:T(1024)(128)(2,1)S(1)}, bf16[768]{0:T(1024)(128)(2,1)}, u32[]{:S(2)}) copy-start(bf16[768]{0:T(1024)(128)(2,1)} %param.21) | copy-start | bytes 4612
  79.7 49.0 %copy-start.40 = (bf16[768]{0:T(1024)(128)(2,1)S(1)}, bf16[768]{0:T(1024)(128)(2,1)}, u32[]{:S(2)}) copy-start(bf16[768]{0:T(1024)(128)(2,1)} %param.22) | copy-start | bytes 4612
  79.7 49.0 %copy-start.41 = (bf16[768]{0:T(1024)(128)(2,1)S(1)}, bf16[768]{0:T(1024)(128)(2,1)}, u32[]{:S(2)}) copy-start(bf16[768]{0:T(1024)(128)(2,1)} %param.26) | copy-start | bytes 4612
  79.7 49.0 %copy-start.42 = (bf16[768]{0:T(1024)(128)(2,1)S(1)}, bf16[768]{0:T(1024)(128)(2,1)}, u32[]{:S(2)}) copy-start(bf16[768]{0:T(1024)(128)(2,1)} %param.27) | copy-start | bytes 4612
  79.7 49.0 %copy-start.43 = (bf16[768]{0:T(1024)(128)(2,1)S(1)}, bf16[768]{0:T(1024)(128)(2,1)}, u32[]{:S(2)}) copy-start(bf16[768]{0:T(1024)(128)(2,1)} %param.28) | copy-start | bytes 4612
  79.8 49.7 %copy-start.28 = (bf16[1,1,2,768]{3,1,2,0:T(2,128)(2,1)S(1)}, bf16[1,1,2,768]{3,1,2,0:T(2,128)(2,1)}, u32[]{:S(2)}) copy-start(bf16[1,1,2,768]{3,1,2,0:T(2,128)(2,1)} %copy-done.27) | copy-start | bytes 9220
  79.8 49.7 %copy-start.30 = (bf16[1,1,2,768]{3,1,2,0:T(2,128)(2,1)S(1)}, bf16[1,1,2,768]{3,1,2,0:T(2,128)(2,1)}, u32[]{:S(2)}) copy-start(bf16[1,1,2,768]{3,1,2,0:T(2,128)(2,1)} %copy-done.29) | copy-start | bytes 9220
  79.8 49.7 %copy-start.32 = (bf16[1,1,2,768]{3,1,2,0:T(2,128)(2,1)S(1)}, bf16[1,1,2,768]{3,1,2,0:T(2,128)(2,1)}, u32[]{:S(2)}) copy-start(bf16[1,1,2,768]{3,1,2,0:T(2,128)(2,1)} %copy-done.31) | copy-start | bytes 9220
  128.0 3.0 collective-permute-start.19
  128.1 4.8 %collective-permute-start.20 = (bf16[3,96,1536]{2,1,0:T(8,128)(2,1)}, bf16[3,96,1536]{2,1,0:T(8,128)(2,1)S(1)}, u32[]{:S(2)}, u32[]{:S(2)}) collective-permute-start(bf16[3,96,1536]{2,1,0:T(8,128)(2,1)} %collective-permute-done.11.refs_2_), channel_id=1, source_target_pairs={{0,4},{4,0},{8,12},{12,8},{16,20},{20,16},{24,28},{28,24},{1,5},{5... | collective-permute-start | bytes 2654216 | tf_op jit(solution)/shard_map/ppermute | solution.py:438
  128.6 4.8 %collective-permute-start.21 = (bf16[3,96,1536]{2,1,0:T(8,128)(2,1)}, bf16[3,96,1536]{2,1,0:T(8,128)(2,1)}, u32[]{:S(2)}, u32[]{:S(2)}) collective-permute-start(bf16[3,96,1536]{2,1,0:T(8,128)(2,1)} %collective-permute-done.12.refs_3_), channel_id=1, source_target_pairs={{0,4},{4,0},{8,12},{12,8},{16,20},{20,16},{24,28},{28,24},{1,5},{5... | collective-permute-start | bytes 2654216 | tf_op jit(solution)/shard_map/ppermute | solution.py:438
  201.5 13.4 %collective-permute-start.22 = (bf16[2,2,4,96,960]{4,3,2,1,0:T(8,128)(2,1)}, bf16[2,2,4,96,960]{4,3,2,1,0:T(8,128)(2,1)S(1)}, u32[]{:S(2)}, u32[]{:S(2)}) collective-permute-start(bf16[2,2,4,96,960]{4,3,2,1,0:T(8,128)(2,1)} %get-tuple-element.152), channel_id=1, source_target_pairs={{0,4},{4,0},{8,12},{12,8},{16,20},{20,16},{24,28},{28,24},{1,5},{5... | collective-permute-start | bytes 8847368 | tf_op jit(solution)/shard_map/ppermute | solution.py:438
  216.6 5.9 %collective-permute-start.23 = (bf16[2,2,4,104,768]{4,3,2,1,0:T(8,128)(2,1)}, bf16[2,2,4,104,768]{4,3,2,1,0:T(8,128)(2,1)S(1)}, u32[]{:S(2)}, u32[]{:S(2)}) collective-permute-start(bf16[2,2,4,104,768]{4,3,2,1,0:T(8,128)(2,1)} %get-tuple-element.160), channel_id=1, source_target_pairs={{0,4},{4,0},{8,12},{12,8},{16,20},{20,16},{24,28},{28,24},{1,5},{5... | collective-permute-start | bytes 7667720 | tf_op jit(solution)/shard_map/ppermute | solution.py:438
  222.5 37.0 %collective-permute-start.24 = (bf16[2,4,96,960]{3,2,1,0:T(8,128)(2,1)}, bf16[2,4,96,960]{3,2,1,0:T(8,128)(2,1)}, u32[]{:S(2)}, u32[]{:S(2)}) collective-permute-start(bf16[2,4,96,960]{3,2,1,0:T(8,128)(2,1)} %get-tuple-element.253), channel_id=1, source_target_pairs={{0,16},{4,20},{8,24},{12,28},{16,0},{20,4},{24,8},{28,12},{1,17},{... | collective-permute-start | bytes 4423688 | tf_op jit(solution)/shard_map/ppermute | solution.py:438
  224.2 35.3 %collective-permute-start.25 = (bf16[2,4,104,768]{3,2,1,0:T(8,128)(2,1)}, bf16[2,4,104,768]{3,2,1,0:T(8,128)(2,1)}, u32[]{:S(2)}, u32[]{:S(2)}) collective-permute-start(bf16[2,4,104,768]{3,2,1,0:T(8,128)(2,1)} %get-tuple-element.256), channel_id=1, source_target_pairs={{0,8},{4,12},{8,0},{12,4},{16,24},{20,28},{24,16},{28,20},{1,9},{5... | collective-permute-start | bytes 3833864 | tf_op jit(solution)/shard_map/ppermute | solution.py:438
  272.5 20.3 %collective-permute-start.28 = (bf16[2,2,2,104,576]{4,3,2,1,0:T(8,128)(2,1)}, bf16[2,2,2,104,576]{4,3,2,1,0:T(8,128)(2,1)S(1)}, u32[]{:S(2)}, u32[]{:S(2)}) collective-permute-start(bf16[2,2,2,104,576]{4,3,2,1,0:T(8,128)(2,1)} %get-tuple-element.181), channel_id=1, source_target_pairs={{0,4},{4,0},{8,12},{12,8},{16,20},{20,16},{24,28},{28,24},{1,5},{5... | collective-permute-start | bytes 2875400 | tf_op jit(solution)/shard_map/ppermute | solution.py:438
  272.5 20.3 %collective-permute-start.26 = (bf16[4,96,960]{2,1,0:T(8,128)(2,1)}, bf16[4,96,960]{2,1,0:T(8,128)(2,1)}, u32[]{:S(2)}, u32[]{:S(2)}) collective-permute-start(bf16[4,96,960]{2,1,0:T(8,128)(2,1)} %get-tuple-element.257), channel_id=1, source_target_pairs={{0,8},{4,12},{8,0},{12,4},{16,24},{20,28},{24,16},{28,20},{1,9},{5... | collective-permute-start | bytes 2211848 | tf_op jit(solution)/shard_map/ppermute | solution.py:438
  273.1 18.3 %collective-permute-start.27 = (bf16[4,104,768]{2,1,0:T(8,128)(2,1)}, bf16[4,104,768]{2,1,0:T(8,128)(2,1)}, u32[]{:S(2)}, u32[]{:S(2)}) collective-permute-start(bf16[4,104,768]{2,1,0:T(8,128)(2,1)} %get-tuple-element.260), channel_id=1, source_target_pairs={{0,16},{4,20},{8,24},{12,28},{16,0},{20,4},{24,8},{28,12},{1,17},{... | collective-permute-start | bytes 1916936 | tf_op jit(solution)/shard_map/ppermute | solution.py:438
  274.9 17.9 %copy-start.11 = (bf16[2,2,2,104,576]{4,3,2,1,0:T(8,128)(2,1)S(1)}, bf16[2,2,2,104,576]{4,3,2,1,0:T(8,128)(2,1)}, u32[]{:S(2)}) copy-start(bf16[2,2,2,104,576]{4,3,2,1,0:T(8,128)(2,1)} %get-tuple-element.192) | copy-start | bytes 2875396
  294.1 26.4 %collective-permute-start.31 = (bf16[2,2,104,576]{3,2,1,0:T(8,128)(2,1)}, bf16[2,2,104,576]{3,2,1,0:T(8,128)(2,1)}, u32[]{:S(2)}, u32[]{:S(2)}) collective-permute-start(bf16[2,2,104,576]{3,2,1,0:T(8,128)(2,1)} %get-tuple-element.264), channel_id=1, source_target_pairs={{0,8},{4,12},{8,0},{12,4},{16,24},{20,28},{24,16},{28,20},{1,9},{5... | collective-permute-start | bytes 1437704 | tf_op jit(solution)/shard_map/ppermute | solution.py:438
  298.3 22.2 %collective-permute-start.30 = (bf16[104,1728]{1,0:T(8,128)(2,1)}, bf16[104,1728]{1,0:T(8,128)(2,1)S(1)}, u32[]{:S(2)}, u32[]{:S(2)}) collective-permute-start(bf16[104,1728]{1,0:T(8,128)(2,1)} %fusion.23), channel_id=1, source_target_pairs={{0,3},{1,0},{2,1},{3,2},{4,7},{5,4},{6,5},{7,6},{8,11},{9,8},{10,9... | collective-permute-start | bytes 1078280 | tf_op jit(solution)/shard_map/ppermute | solution.py:434
  302.7 17.8 %collective-permute-start.29 = (bf16[104,1728]{1,0:T(8,128)(2,1)}, bf16[104,1728]{1,0:T(8,128)(2,1)S(1)}, u32[]{:S(2)}, u32[]{:S(2)}) collective-permute-start(bf16[104,1728]{1,0:T(8,128)(2,1)} %fusion.22), channel_id=1, source_target_pairs={{0,1},{1,2},{2,3},{3,0},{4,5},{5,6},{6,7},{7,4},{8,9},{9,10},{10,1... | collective-permute-start | bytes 1078280 | tf_op jit(solution)/shard_map/ppermute | solution.py:434
  302.8 17.7 %copy-start.2 = (bf16[1,3,3,64,1536]{4,3,2,1,0:T(8,128)(2,1)S(1)}, bf16[1,3,3,64,1536]{4,3,2,1,0:T(8,128)(2,1)}, u32[]{:S(2)}) copy-start(bf16[1,3,3,64,1536]{4,3,2,1,0:T(8,128)(2,1)} %get-tuple-element.189) | copy-start | bytes 5308420
  332.9 20.0 %collective-permute-start.34 = (bf16[2,2,2,104,576]{4,3,2,1,0:T(8,128)(2,1)}, bf16[2,2,2,104,576]{4,3,2,1,0:T(8,128)(2,1)S(1)}, u32[]{:S(2)}, u32[]{:S(2)}) collective-permute-start(bf16[2,2,2,104,576]{4,3,2,1,0:T(8,128)(2,1)} %get-tuple-element.209), channel_id=1, source_target_pairs={{0,4},{4,0},{8,12},{12,8},{16,20},{20,16},{24,28},{28,24},{1,5},{5... | collective-permute-start | bytes 2875400 | tf_op jit(solution)/shard_map/ppermute | solution.py:438
  332.9 20.0 %collective-permute-start.33 = (bf16[104,1728]{1,0:T(8,128)(2,1)S(1)}, bf16[104,1728]{1,0:T(8,128)(2,1)S(1)}, u32[]{:S(2)}, u32[]{:S(2)}) collective-permute-start(bf16[104,1728]{1,0:T(8,128)(2,1)S(1)} %fusion.25), channel_id=1, source_target_pairs={{0,2},{1,3},{2,0},{3,1},{4,6},{5,7},{6,4},{7,5},{8,10},{9,11},{10,... | collective-permute-start | bytes 1078280 | tf_op jit(solution)/shard_map/ppermute | solution.py:434
  334.8 8.5 %collective-permute-start.32 = (bf16[2,104,576]{2,1,0:T(8,128)(2,1)S(1)}, bf16[2,104,576]{2,1,0:T(8,128)(2,1)S(1)}, u32[]{:S(2)}, u32[]{:S(2)}) collective-permute-start(bf16[2,104,576]{2,1,0:T(8,128)(2,1)S(1)} %get-tuple-element.276), channel_id=1, source_target_pairs={{0,16},{4,20},{8,24},{12,28},{16,0},{20,4},{24,8},{28,12},{1,17},{... | collective-permute-start | bytes 718856 | tf_op jit(solution)/shard_map/ppermute | solution.py:438
  354.4 30.9 %collective-permute-start.35 = (bf16[2,2,104,576]{3,2,1,0:T(8,128)(2,1)S(1)}, bf16[2,2,104,576]{3,2,1,0:T(8,128)(2,1)S(1)}, u32[]{:S(2)}, u32[]{:S(2)}) collective-permute-start(bf16[2,2,104,576]{3,2,1,0:T(8,128)(2,1)S(1)} %get-tuple-element.261), channel_id=1, source_target_pairs={{0,8},{4,12},{8,0},{12,4},{16,24},{20,28},{24,16},{28,20},{1,9},{5... | collective-permute-start | bytes 1437704 | tf_op jit(solution)/shard_map/ppermute | solution.py:438
  354.9 23.8 %collective-permute-start.36 = (bf16[104,1728]{1,0:T(8,128)(2,1)S(1)}, bf16[104,1728]{1,0:T(8,128)(2,1)S(1)}, u32[]{:S(2)}, u32[]{:S(2)}) collective-permute-start(bf16[104,1728]{1,0:T(8,128)(2,1)S(1)} %add_convert_fusion.8), channel_id=1, source_target_pairs={{0,8},{4,12},{8,0},{12,4},{16,24},{20,28},{24,16},{28,20},{1,9},{5... | collective-permute-start | bytes 1078280 | tf_op jit(solution)/shard_map/ppermute | solution.py:438
  356.7 22.0 %collective-permute-start.37 = (bf16[104,1728]{1,0:T(8,128)(2,1)S(1)}, bf16[104,1728]{1,0:T(8,128)(2,1)S(1)}, u32[]{:S(2)}, u32[]{:S(2)}) collective-permute-start(bf16[104,1728]{1,0:T(8,128)(2,1)S(1)} %add_convert_fusion.8), channel_id=1, source_target_pairs={{0,16},{4,20},{8,24},{12,28},{16,0},{20,4},{24,8},{28,12},{1,17},{... | collective-permute-start | bytes 1078280 | tf_op jit(solution)/shard_map/ppermute | solution.py:438
  358.5 26.8 %collective-permute-start.38 = (bf16[104,1728]{1,0:T(8,128)(2,1)S(1)}, bf16[104,1728]{1,0:T(8,128)(2,1)S(1)}, u32[]{:S(2)}, u32[]{:S(2)}) collective-permute-start(bf16[104,1728]{1,0:T(8,128)(2,1)S(1)} %add_convert_fusion.8), channel_id=1, source_target_pairs={{0,24},{4,28},{8,16},{12,20},{16,8},{20,12},{24,0},{28,4},{1,25},{... | collective-permute-start | bytes 1078280 | tf_op jit(solution)/shard_map/ppermute | solution.py:438
  358.5 6.9 %collective-permute-start.39 = (bf16[104,576]{1,0:T(8,128)(2,1)S(1)}, bf16[104,576]{1,0:T(8,128)(2,1)S(1)}, u32[]{:S(2)}, u32[]{:S(2)}) collective-permute-start(bf16[104,576]{1,0:T(8,128)(2,1)S(1)} %get-tuple-element.278), channel_id=1, source_target_pairs={{0,1},{1,2},{2,3},{3,0},{4,5},{5,6},{6,7},{7,4},{8,9},{9,10},{10,1... | collective-permute-start | bytes 359432 | tf_op jit(solution)/shard_map/ppermute | solution.py:434
  365.4 13.3 %collective-permute-start.40 = (bf16[104,576]{1,0:T(8,128)(2,1)S(1)}, bf16[104,576]{1,0:T(8,128)(2,1)S(1)}, u32[]{:S(2)}, u32[]{:S(2)}) collective-permute-start(bf16[104,576]{1,0:T(8,128)(2,1)S(1)} %get-tuple-element.277), channel_id=1, source_target_pairs={{0,2},{1,3},{2,0},{3,1},{4,6},{5,7},{6,4},{7,5},{8,10},{9,11},{10,... | collective-permute-start | bytes 359432 | tf_op jit(solution)/shard_map/ppermute | solution.py:434
  385.4 22.0 %copy-start.3 = (bf16[4,104,1728]{2,1,0:T(8,128)(2,1)}, bf16[4,104,1728]{2,1,0:T(8,128)(2,1)S(1)}, u32[]{:S(2)}) copy-start(bf16[4,104,1728]{2,1,0:T(8,128)(2,1)S(1)} %pad_maximum_fusion.1.x) | copy-start | bytes 4313092
  385.4 9.1 %collective-permute-start.42 = (bf16[4,104,1728]{2,1,0:T(8,128)(2,1)S(1)}, bf16[4,104,1728]{2,1,0:T(8,128)(2,1)S(1)}, u32[]{:S(2)}, u32[]{:S(2)}) collective-permute-start(bf16[4,104,1728]{2,1,0:T(8,128)(2,1)S(1)} %pad_maximum_fusion.1.x), channel_id=1, source_target_pairs={{0,4},{4,0},{8,12},{12,8},{16,20},{20,16},{24,28},{28,24},{1,5},{5... | collective-permute-start | bytes 4313096 | tf_op jit(solution)/shard_map/ppermute | solution.py:438
  385.7 8.9 %collective-permute-start.41 = (bf16[2,104,576]{2,1,0:T(8,128)(2,1)S(1)}, bf16[2,104,576]{2,1,0:T(8,128)(2,1)S(1)}, u32[]{:S(2)}, u32[]{:S(2)}) collective-permute-start(bf16[2,104,576]{2,1,0:T(8,128)(2,1)S(1)} %get-tuple-element.273), channel_id=1, source_target_pairs={{0,16},{4,20},{8,24},{12,28},{16,0},{20,4},{24,8},{28,12},{1,17},{... | collective-permute-start | bytes 718856 | tf_op jit(solution)/shard_map/ppermute | solution.py:438
  394.6 5.2 %collective-permute-start.43 = (bf16[104,576]{1,0:T(8,128)(2,1)S(1)}, bf16[104,576]{1,0:T(8,128)(2,1)S(1)}, u32[]{:S(2)}, u32[]{:S(2)}) collective-permute-start(bf16[104,576]{1,0:T(8,128)(2,1)S(1)} %fusion.53), channel_id=1, source_target_pairs={{0,3},{1,0},{2,1},{3,2},{4,7},{5,4},{6,5},{7,6},{8,11},{9,8},{10,9... | collective-permute-start | bytes 359432 | tf_op jit(solution)/shard_map/ppermute | solution.py:434
  399.9 5.8 %collective-permute-start.44 = (bf16[104,576]{1,0:T(8,128)(2,1)S(1)}, bf16[104,576]{1,0:T(8,128)(2,1)S(1)}, u32[]{:S(2)}, u32[]{:S(2)}) collective-permute-start(bf16[104,576]{1,0:T(8,128)(2,1)S(1)} %fusion.36), channel_id=1, source_target_pairs={{0,8},{4,12},{8,0},{12,4},{16,24},{20,28},{24,16},{28,20},{1,9},{5... | collective-permute-start | bytes 359432 | tf_op jit(solution)/shard_map/ppermute | solution.py:438
  400.3 5.6 %collective-permute-start.45 = (bf16[104,576]{1,0:T(8,128)(2,1)S(1)}, bf16[104,576]{1,0:T(8,128)(2,1)S(1)}, u32[]{:S(2)}, u32[]{:S(2)}) collective-permute-start(bf16[104,576]{1,0:T(8,128)(2,1)S(1)} %fusion.36), channel_id=1, source_target_pairs={{0,16},{4,20},{8,24},{12,28},{16,0},{20,4},{24,8},{28,12},{1,17},{... | collective-permute-start | bytes 359432 | tf_op jit(solution)/shard_map/ppermute | solution.py:438
  401.2 6.2 %collective-permute-start.46 = (bf16[104,576]{1,0:T(8,128)(2,1)S(1)}, bf16[104,576]{1,0:T(8,128)(2,1)S(1)}, u32[]{:S(2)}, u32[]{:S(2)}) collective-permute-start(bf16[104,576]{1,0:T(8,128)(2,1)S(1)} %fusion.36), channel_id=1, source_target_pairs={{0,24},{4,28},{8,16},{12,20},{16,8},{20,12},{24,0},{28,4},{1,25},{... | collective-permute-start | bytes 359432 | tf_op jit(solution)/shard_map/ppermute | solution.py:438
  407.5 7.1 %collective-permute-start.47 = (bf16[4,104,576]{2,1,0:T(8,128)(2,1)S(1)}, bf16[4,104,576]{2,1,0:T(8,128)(2,1)S(1)}, u32[]{:S(2)}, u32[]{:S(2)}) collective-permute-start(bf16[4,104,576]{2,1,0:T(8,128)(2,1)S(1)} %pad_maximum_fusion.4.x), channel_id=1, source_target_pairs={{0,4},{4,0},{8,12},{12,8},{16,20},{20,16},{24,28},{28,24},{1,5},{5... | collective-permute-start | bytes 1437704 | tf_op jit(solution)/shard_map/ppermute | solution.py:438
  (29 other events, 134.2 us)
